TPU v7x, 32 devices: a whole 2x2x4 slice. The times are simulated.
32 devices in a mesh: dp: 4 (over x, core), seq: 8 (over z, y).
Axes of the slice: x: 2, y: 2, z: 4, core: 2. Of those that a mesh axis runs over, the one named last changes fastest.
Arguments:
- tokens: bfloat16 [2048, 4, 768], P('seq', 'dp'), may hold values from -6 to 6
- memory: bfloat16 [1536, 4, 768], P(None, 'dp'), may hold values from -6 to 6
- piece_starts: int32 [4, 3], P('dp'), may hold values from 0 to 1792, as said below
- memory_lengths: int32 [4], P('dp'), may hold values from 384 to 1536, as said below
- self_gain: bfloat16 [768], P(('dp', 'seq')), may hold values from 0.25 to 1.75
- self_shift: bfloat16 [768], P(('dp', 'seq')), may hold values from -3 to 3
- query_weight: bfloat16 [768, 768], P(('dp', 'seq')), may hold values from -0.21875 to 0.21875
- query_bias: bfloat16 [768], P(('dp', 'seq')), may hold values from -3 to 3
- key_weight: bfloat16 [768, 768], P(('dp', 'seq')), may hold values from -0.21875 to 0.21875
- value_weight: bfloat16 [768, 768], P(('dp', 'seq')), may hold values from -0.21875 to 0.21875
- value_bias: bfloat16 [768], P(('dp', 'seq')), may hold values from -3 to 3
- attn_out_weight: bfloat16 [768, 768], P(('dp', 'seq')), may hold values from -0.875 to 0.875
- attn_out_bias: bfloat16 [768], P(('dp', 'seq')), may hold values from -3 to 3
- cross_gain: bfloat16 [768], P(('dp', 'seq')), may hold values from 0.25 to 1.75
- cross_shift: bfloat16 [768], P(('dp', 'seq')), may hold values from -3 to 3
- cross_query_weight: bfloat16 [768, 768], P(('dp', 'seq')), may hold values from -0.21875 to 0.21875
- cross_query_bias: bfloat16 [768], P(('dp', 'seq')), may hold values from -3 to 3
- cross_key_weight: bfloat16 [768, 768], P(('dp', 'seq')), may hold values from -0.21875 to 0.21875
- cross_value_weight: bfloat16 [768, 768], P(('dp', 'seq')), may hold values from -0.21875 to 0.21875
- cross_value_bias: bfloat16 [768], P(('dp', 'seq')), may hold values from -3 to 3
- cross_out_weight: bfloat16 [768, 768], P(('dp', 'seq')), may hold values from -0.875 to 0.875
- cross_out_bias: bfloat16 [768], P(('dp', 'seq')), may hold values from -3 to 3
- mlp_gain: bfloat16 [768], P(('dp', 'seq')), may hold values from 0.25 to 1.75
- mlp_shift: bfloat16 [768], P(('dp', 'seq')), may hold values from -3 to 3
- fc_in_weight: bfloat16 [768, 3072], P(('dp', 'seq')), may hold values from -0.21875 to 0.21875
- fc_in_bias: bfloat16 [3072], P(('dp', 'seq')), may hold values from -3 to 3
- fc_out_weight: bfloat16 [3072, 768], P(('dp', 'seq')), may hold values from -0.109375 to 0.109375
- fc_out_bias: bfloat16 [768], P(('dp', 'seq')), may hold values from -3 to 3
- out_grad: float32 [2048, 4, 768], P('seq', 'dp'), may hold values from -6 to 6
Outputs:
- output: bfloat16 [2048, 4, 768], P('seq', 'dp')
- token_grad: float32 [2048, 4, 768], P('seq', 'dp')
- memory_grad: float32 [1536, 4, 768], P(None, 'dp')
- grad_self_gain: float32 [768], P(('dp', 'seq'))
- grad_self_shift: float32 [768], P(('dp', 'seq'))
- grad_query_weight: float32 [768, 768], P(('dp', 'seq'))
- grad_query_bias: float32 [768], P(('dp', 'seq'))
- grad_key_weight: float32 [768, 768], P(('dp', 'seq'))
- grad_value_weight: float32 [768, 768], P(('dp', 'seq'))
- grad_value_bias: float32 [768], P(('dp', 'seq'))
- grad_attn_out_weight: float32 [768, 768], P(('dp', 'seq'))
- grad_attn_out_bias: float32 [768], P(('dp', 'seq'))
- grad_cross_gain: float32 [768], P(('dp', 'seq'))
- grad_cross_shift: float32 [768], P(('dp', 'seq'))
- grad_cross_query_weight: float32 [768, 768], P(('dp', 'seq'))
- grad_cross_query_bias: float32 [768], P(('dp', 'seq'))
- grad_cross_key_weight: float32 [768, 768], P(('dp', 'seq'))
- grad_cross_value_weight: float32 [768, 768], P(('dp', 'seq'))
- grad_cross_value_bias: float32 [768], P(('dp', 'seq'))
- grad_cross_out_weight: float32 [768, 768], P(('dp', 'seq'))
- grad_cross_out_bias: float32 [768], P(('dp', 'seq'))
- grad_mlp_gain: float32 [768], P(('dp', 'seq'))
- grad_mlp_shift: float32 [768], P(('dp', 'seq'))
- grad_fc_in_weight: float32 [768, 3072], P(('dp', 'seq'))
- grad_fc_in_bias: float32 [3072], P(('dp', 'seq'))
- grad_fc_out_weight: float32 [3072, 768], P(('dp', 'seq'))
- grad_fc_out_bias: float32 [768], P(('dp', 'seq'))
Inputs may be any that keep to these rules, and one draw needn't show every extreme that they name: `piece_starts`: each sequence has 3 audio-prompt pieces of 256 positions; each starts at a multiple of 128, the pieces of one sequence don't intersect and each lies inside the sequence. `memory_lengths`: frames at or beyond a sequence's length are padding; some sequence uses all 1536 frames.
All inputs are finite; a program needn't handle non-finite values.
Results may differ from a plain program's by a relative error of at most 0.035.
Values may be sent and summed in bfloat16 or wider, within the bound.
No kernel may reach another device: no remote copies, remote signals or barrier semaphores. Data moves between devices by JAX's collectives and lax.ppermute only.
A program may use at most 256 MiB of HBM per device.

v0:
```python
import math

import jax
import jax.numpy as jnp
from jax import lax
from jax.experimental import pallas as pl
from jax.experimental.pallas import tpu as pltpu
from jax.sharding import PartitionSpec as P


D = 768
HEADS = 12
HEAD = 64
PIECE = 256


norm_epsilon = 1e-05
neg_large = -1e30


def rounded(tensor):
    return tensor.astype(jnp.bfloat16)


def project(left_rows, matrix):
    return jnp.dot(left_rows, matrix, preferred_element_type=jnp.float32)


def project_back(left_rows, matrix):
    return lax.dot_general(
        left_rows, matrix, (((1,), (1,)), ((), ())), preferred_element_type=jnp.float32
    )


def weight_grad(inputs, grad_rows):
    return lax.dot_general(
        inputs, grad_rows, (((0,), (0,)), ((), ())), preferred_element_type=jnp.float32
    )


def column_sums(grad_rows):
    return jnp.sum(grad_rows.astype(jnp.float32), axis=0)


def exact_gelu(inputs):
    return jax.nn.gelu(inputs, approximate=False)


def norm_forward(token_rows, norm_gain, norm_shift):
    centre = token_rows - jnp.mean(token_rows, axis=-1, keepdims=True)
    inverse = lax.rsqrt(jnp.mean(centre * centre, axis=-1, keepdims=True) + norm_epsilon)
    scaled = centre * inverse
    return (scaled * norm_gain + norm_shift, scaled, inverse)


def norm_backward(grad_normed, scaled, inverse, norm_gain):
    grad_scaled = grad_normed * norm_gain
    mean_grad = jnp.mean(grad_scaled, axis=-1, keepdims=True)
    mean_cross = jnp.mean(grad_scaled * scaled, axis=-1, keepdims=True)
    grad_input = inverse * (grad_scaled - mean_grad - scaled * mean_cross)
    return (grad_input, jnp.sum(grad_normed * scaled, axis=0), jnp.sum(grad_normed, axis=0))


def piece_labels(positions, starts):
    inside = (positions[None, :, None] >= starts[:, None, :]) & (
        positions[None, :, None] < starts[:, None, :] + PIECE
    )
    numbers = jnp.arange(1, starts.shape[1] + 1, dtype=jnp.int32)
    return jnp.sum(jnp.where(inside, numbers, 0), axis=2)


def visible(query_pos, query_label, key_pos, key_label):
    causal = (key_pos[None, :] <= query_pos[:, None])[:, None, :]
    query_side = jnp.transpose(query_label)[:, :, None]
    same_piece = (query_side == key_label[None, :, :]) & (query_side > 0)
    return (causal | same_piece)[:, :, None, :]


PAIR = 2 * HEAD
QUERY_BLOCK = 256
KEY_BLOCK = 512


def to_pairs(rows, seq_count):
    blocks = jnp.transpose(rows.reshape(rows.shape[0], D // PAIR, PAIR), (1, 0, 2))
    return jnp.pad(blocks, ((0, seq_count - D // PAIR), (0, 0), (0, 0)))


def from_pairs(blocks):
    kept = blocks[: D // PAIR]
    return jnp.transpose(kept, (1, 0, 2)).reshape(kept.shape[1], D)


def dot_rows(left, right):
    return lax.dot_general(left, right, (((1,), (1,)), ((), ())), preferred_element_type=jnp.float32)


def dot_plain(left, right):
    return lax.dot_general(left, right, (((1,), (0,)), ((), ())), preferred_element_type=jnp.float32)


def dot_columns(left, right):
    return lax.dot_general(left, right, (((0,), (0,)), ((), ())), preferred_element_type=jnp.float32)


def split_pair(block):
    lanes = lax.broadcasted_iota(jnp.int32, block.shape, 1)
    zero = jnp.zeros_like(block)
    return (jnp.where(lanes < HEAD, block, zero), jnp.where(lanes < HEAD, zero, block))


def join_pair(first, second, shape):
    lanes = lax.broadcasted_iota(jnp.int32, shape, 1)
    return jnp.where(lanes < HEAD, first, second)


def stack_pair(block):
    return jnp.concatenate(split_pair(block), axis=0)


def join_stack(stacked):
    rows = stacked.shape[0] // 2
    return join_pair(stacked[:rows], stacked[rows:], (rows, stacked.shape[1]))


def block_allowed(query_pos, key_pos, query_label, key_label):
    same_piece = (query_label == key_label) & (query_label > 0)
    return (key_pos <= query_pos) | same_piece


def key_block_range(block, key_rows):
    full = block * QUERY_BLOCK // KEY_BLOCK
    last = ((block + 2) * QUERY_BLOCK + KEY_BLOCK - 1) // KEY_BLOCK
    return (full, jnp.minimum(last, key_rows // KEY_BLOCK))


def self_forward_body(query_ref, key_ref, value_ref, column_ref, row_ref, out_ref, log_ref):
    block = pl.program_id(0)
    queries = stack_pair(query_ref[...] * jnp.bfloat16(0.125))
    query_label = column_ref[...]

    def step(key_block, state, masked):
        start = pl.multiple_of(key_block * KEY_BLOCK, KEY_BLOCK)
        here = pl.ds(start, KEY_BLOCK)
        row_max, row_total, weighted = state
        scores = dot_rows(queries, key_ref[here, :])
        if masked:
            shape = (QUERY_BLOCK, KEY_BLOCK)
            allowed = block_allowed(
                block * QUERY_BLOCK + lax.broadcasted_iota(jnp.int32, shape, 0),
                start + lax.broadcasted_iota(jnp.int32, shape, 1),
                query_label,
                row_ref[:, here],
            )
            scores = jnp.concatenate(
                (
                    jnp.where(allowed, scores[:QUERY_BLOCK], neg_large),
                    jnp.where(allowed, scores[QUERY_BLOCK:], neg_large),
                ),
                axis=0,
            )
        new_max = jnp.maximum(row_max, jnp.max(scores, axis=1, keepdims=True))
        exp_terms = jnp.exp(scores - new_max)
        factor = jnp.exp(row_max - new_max)
        row_total = row_total * factor + jnp.sum(exp_terms, axis=1, keepdims=True)
        weighted = weighted * factor + dot_plain(rounded(exp_terms), value_ref[here, :])
        return (new_max, row_total, weighted)

    state = (
        jnp.full((2 * QUERY_BLOCK, 1), neg_large, jnp.float32),
        jnp.zeros((2 * QUERY_BLOCK, 1), jnp.float32),
        jnp.zeros((2 * QUERY_BLOCK, PAIR), jnp.float32),
    )
    full, last = key_block_range(block, key_ref.shape[0])
    state = lax.fori_loop(0, full, lambda index, state: step(index, state, False), state)
    state = lax.fori_loop(full, last, lambda index, state: step(index, state, True), state)
    row_max, row_total, weighted = state
    out_ref[...] = join_stack(weighted / row_total)
    log_ref[...] = join_stack(jnp.broadcast_to(row_max + jnp.log(row_total), weighted.shape))


def self_forward(queries, keys, values, labels):
    length = queries.shape[0]
    block_spec = pl.BlockSpec((QUERY_BLOCK, PAIR), lambda index: (index, 0))
    whole_spec = pl.BlockSpec((length, PAIR), lambda index: (0, 0))
    result = jax.ShapeDtypeStruct((length, PAIR), jnp.float32)
    return pl.pallas_call(
        self_forward_body,
        grid=(length // QUERY_BLOCK,),
        in_specs=[
            block_spec,
            whole_spec,
            whole_spec,
            pl.BlockSpec((QUERY_BLOCK, 1), lambda index: (index, 0)),
            pl.BlockSpec((1, length), lambda index: (0, 0)),
        ],
        out_specs=[block_spec, block_spec],
        out_shape=[result, result],
        name="self_forward",
    )(queries, keys, values, labels[:, None], labels[None, :])


def self_backward_body(
    query_ref,
    key_ref,
    value_ref,
    column_ref,
    row_ref,
    out_ref,
    log_ref,
    grad_ref,
    grad_query_ref,
    grad_key_ref,
    grad_value_ref,
    key_sum,
    value_sum,
):
    block = pl.program_id(0)
    block_count = pl.num_programs(0)

    @pl.when(block == 0)
    def clear():
        key_sum[...] = jnp.zeros_like(key_sum)
        value_sum[...] = jnp.zeros_like(value_sum)

    queries = stack_pair(query_ref[...] * jnp.bfloat16(0.125))
    query_label = row_ref[...]
    grad_rows = grad_ref[...]
    grads = stack_pair(grad_rows)
    products = stack_pair(grad_rows.astype(jnp.float32) * out_ref[...])
    delta = jnp.sum(jnp.transpose(products), axis=0, keepdims=True)
    log_columns = jnp.transpose(log_ref[...])
    logs = jnp.concatenate((log_columns[:1], log_columns[HEAD : HEAD + 1]), axis=1)

    def step(key_block, query_sum, masked):
        start = pl.multiple_of(key_block * KEY_BLOCK, KEY_BLOCK)
        here = pl.ds(start, KEY_BLOCK)
        keys = key_ref[here, :]
        scores = dot_rows(keys, queries)
        if masked:
            shape = (KEY_BLOCK, QUERY_BLOCK)
            allowed = block_allowed(
                block * QUERY_BLOCK + lax.broadcasted_iota(jnp.int32, shape, 1),
                start + lax.broadcasted_iota(jnp.int32, shape, 0),
                query_label,
                column_ref[here, :],
            )
            scores = jnp.concatenate(
                (
                    jnp.where(allowed, scores[:, :QUERY_BLOCK], neg_large),
                    jnp.where(allowed, scores[:, QUERY_BLOCK:], neg_large),
                ),
                axis=1,
            )
        probs = jnp.exp(scores - logs)
        grad_probs = dot_rows(value_ref[here, :], grads)
        grad_scores = rounded(probs * (grad_probs - delta))
        key_sum[here, :] = key_sum[here, :] + dot_plain(grad_scores, queries)
        value_sum[here, :] = value_sum[here, :] + dot_plain(rounded(probs), grads)
        return query_sum + dot_columns(grad_scores, keys)

    query_sum = jnp.zeros((2 * QUERY_BLOCK, PAIR), jnp.float32)
    full, last = key_block_range(block, key_ref.shape[0])
    query_sum = lax.fori_loop(0, full, lambda index, total: step(index, total, False), query_sum)
    query_sum = lax.fori_loop(full, last, lambda index, total: step(index, total, True), query_sum)
    grad_query_ref[...] = rounded(join_stack(query_sum) * 0.125)

    @pl.when(block == block_count - 1)
    def finish():
        grad_key_ref[...] = rounded(key_sum[...])
        grad_value_ref[...] = rounded(value_sum[...])


def self_backward(queries, keys, values, labels, attended, log_total, grad_attended):
    length = queries.shape[0]
    block_spec = pl.BlockSpec((QUERY_BLOCK, PAIR), lambda index: (index, 0))
    whole_spec = pl.BlockSpec((length, PAIR), lambda index: (0, 0))
    result = jax.ShapeDtypeStruct((length, PAIR), jnp.bfloat16)
    return pl.pallas_call(
        self_backward_body,
        grid=(length // QUERY_BLOCK,),
        in_specs=[
            block_spec,
            whole_spec,
            whole_spec,
            pl.BlockSpec((length, 1), lambda index: (0, 0)),
            pl.BlockSpec((1, QUERY_BLOCK), lambda index: (0, index)),
            block_spec,
            block_spec,
            block_spec,
        ],
        out_specs=[block_spec, whole_spec, whole_spec],
        out_shape=[result, result, result],
        scratch_shapes=[
            pltpu.VMEM((length, PAIR), jnp.float32),
            pltpu.VMEM((length, PAIR), jnp.float32),
        ],
        name="self_backward",
    )(queries, keys, values, labels[:, None], labels[None, :], attended, log_total, grad_attended)


def widen_body(frame_ref, out_ref):
    parts = D // 128
    for part in range(parts):
        out_ref[pl.ds(part, frame_ref.shape[0], stride=parts), :] = frame_ref[
            :, part * 128 : (part + 1) * 128
        ].astype(jnp.float32)


def widen_frames(frames):
    frame_count = frames.shape[0]
    parts = D // 128
    wide = pl.pallas_call(
        widen_body,
        grid=(6,),
        in_specs=[pl.BlockSpec((frame_count // 6, D), lambda index: (index, 0))],
        out_specs=pl.BlockSpec((frame_count // 6 * parts, 128), lambda index: (index, 0)),
        out_shape=jax.ShapeDtypeStruct((frame_count * parts, 128), jnp.float32),
        name="widen_frames",
    )(frames)
    return wide.reshape(frame_count, 1, D)


def place_rows(vectors, row_count):
    lead = vectors[0].shape[:-1]
    rows = lax.broadcasted_iota(jnp.int32, lead + (row_count, D), len(lead))
    block = jnp.zeros(rows.shape, jnp.bfloat16)
    for slot, vector in enumerate(vectors):
        padding = [(0, 0)] * len(lead) + [(0, D - vector.shape[-1])]
        wide = jnp.pad(vector.astype(jnp.bfloat16), padding)[..., None, :]
        block = jnp.where(rows == slot, wide, block)
    return block


def halve(buffer, axis, axis_name, flip, bit, kind=jnp.bfloat16):
    kept = lax.dynamic_index_in_dim(buffer, bit, axis, keepdims=False)
    sent = lax.dynamic_index_in_dim(buffer, 1 - bit, axis, keepdims=False)
    pairs = [(index, index ^ flip) for index in range(lax.axis_size(axis_name))]
    received = lax.ppermute(sent, axis_name, pairs)
    return (kept.astype(jnp.float32) + received.astype(jnp.float32)).astype(kind)


def frame_mask(length, shape):
    return lax.broadcasted_iota(jnp.int32, shape, 1) < length


def cross_forward_body(length_ref, query_ref, key_ref, value_ref, out_ref, log_ref):
    query_halves = split_pair(query_ref[...])
    value_halves = split_pair(value_ref[...])
    keys = key_ref[...]
    valid = frame_mask(length_ref[0], (query_ref.shape[0], keys.shape[0]))
    attended = jnp.zeros(query_ref.shape, jnp.float32)
    logs = []
    for half in range(2):
        scores = jnp.where(valid, dot_rows(query_halves[half], keys) * 0.125, neg_large)
        row_max = jnp.max(scores, axis=1, keepdims=True)
        exp_terms = jnp.exp(scores - row_max)
        total = jnp.sum(exp_terms, axis=1, keepdims=True)
        attended = attended + dot_plain(rounded(exp_terms), value_halves[half]) / total
        logs.append(row_max + jnp.log(total))
    out_ref[...] = rounded(attended)
    log_ref[...] = join_pair(logs[0], logs[1], log_ref.shape)


def cross_forward(lengths, queries, keys, values):
    query_spec = pl.BlockSpec((queries.shape[0], PAIR), lambda pair: (0, pair))
    frame_spec = pl.BlockSpec((keys.shape[0], PAIR), lambda pair: (0, pair))
    return pl.pallas_call(
        cross_forward_body,
        grid=(D // PAIR,),
        in_specs=[pl.BlockSpec(memory_space=pltpu.SMEM), query_spec, frame_spec, frame_spec],
        out_specs=[query_spec, query_spec],
        out_shape=[
            jax.ShapeDtypeStruct(queries.shape, jnp.bfloat16),
            jax.ShapeDtypeStruct(queries.shape, jnp.float32),
        ],
        name="cross_forward",
    )(lengths, queries, keys, values)


def cross_backward_body(
    length_ref, query_ref, key_ref, value_ref, log_ref, grad_ref, grad_query_ref, grad_frame_ref
):
    query_halves = split_pair(query_ref[...])
    grad_halves = split_pair(grad_ref[...])
    keys = key_ref[...]
    values = value_ref[...]
    key_halves = split_pair(keys)
    valid = frame_mask(length_ref[0], (query_ref.shape[0], keys.shape[0]))
    logs = (log_ref[:, :1], log_ref[:, HEAD : HEAD + 1])
    query_sum = jnp.zeros(query_ref.shape, jnp.float32)
    key_sum = jnp.zeros(keys.shape, jnp.float32)
    value_sum = jnp.zeros(keys.shape, jnp.float32)
    for half in range(2):
        scores = jnp.where(valid, dot_rows(query_halves[half], keys) * 0.125, neg_large)
        probs = jnp.exp(scores - logs[half])
        grad_probs = dot_rows(grad_halves[half], values)
        delta = jnp.sum(probs * grad_probs, axis=1, keepdims=True)
        grad_scores = rounded(probs * (grad_probs - delta) * 0.125)
        query_sum = query_sum + dot_plain(grad_scores, key_halves[half])
        key_sum = key_sum + dot_columns(grad_scores, query_halves[half])
        value_sum = value_sum + dot_columns(rounded(probs), grad_halves[half])
    grad_query_ref[...] = rounded(query_sum)
    grad_frame_ref[0] = rounded(key_sum)
    grad_frame_ref[1] = rounded(value_sum)


def cross_backward(lengths, queries, keys, values, log_total, grad_attended):
    query_spec = pl.BlockSpec((queries.shape[0], PAIR), lambda pair: (0, pair))
    frame_spec = pl.BlockSpec((keys.shape[0], PAIR), lambda pair: (0, pair))
    return pl.pallas_call(
        cross_backward_body,
        grid=(D // PAIR,),
        in_specs=[
            pl.BlockSpec(memory_space=pltpu.SMEM),
            query_spec,
            frame_spec,
            frame_spec,
            query_spec,
            query_spec,
        ],
        out_specs=[
            query_spec,
            pl.BlockSpec((2, keys.shape[0], PAIR), lambda pair: (0, 0, pair)),
        ],
        out_shape=[
            jax.ShapeDtypeStruct(queries.shape, jnp.bfloat16),
            jax.ShapeDtypeStruct((2,) + keys.shape, jnp.bfloat16),
        ],
        name="cross_backward",
    )(lengths, queries, keys, values, log_total, grad_attended)


def local_heads(
    tokens,
    memory,
    piece_starts,
    memory_lengths,
    self_gain,
    self_shift,
    query_weight,
    query_bias,
    key_weight,
    value_weight,
    value_bias,
    attn_out_weight,
    attn_out_bias,
    cross_gain,
    cross_shift,
    cross_query_weight,
    cross_query_bias,
    cross_key_weight,
    cross_value_weight,
    cross_value_bias,
    cross_out_weight,
    cross_out_bias,
    mlp_gain,
    mlp_shift,
    fc_in_weight,
    fc_in_bias,
    fc_out_weight,
    fc_out_bias,
    out_grad,
):
    local_len, batch_count, _ = tokens.shape
    seq_count = lax.axis_size("seq")
    seq_index = lax.axis_index("seq")
    full_length = local_len * seq_count
    token_count = local_len * batch_count
    query_pos = seq_index * local_len + jnp.arange(local_len, dtype=jnp.int32)
    labels = piece_labels(jnp.arange(full_length, dtype=jnp.int32), piece_starts).reshape(-1)
    input_rows = tokens.reshape(token_count, D).astype(jnp.float32)
    shard_rows = query_weight.shape[0]
    wide_parts = fc_in_weight.shape[1] // D
    vector_block = place_rows(
        (
            self_gain,
            self_shift,
            query_bias,
            value_bias,
            attn_out_bias,
            cross_gain,
            cross_shift,
            cross_query_bias,
            cross_value_bias,
            cross_out_bias,
            mlp_gain,
            mlp_shift,
            fc_out_bias,
            fc_in_bias,
        ),
        16,
    )
    fc_in_blocks = jnp.transpose(
        fc_in_weight.reshape(shard_rows, wide_parts, D), (1, 0, 2)
    ).reshape(wide_parts * shard_rows, D)
    first_packed = jnp.concatenate(
        (
            query_weight,
            key_weight,
            value_weight,
            cross_key_weight,
            cross_value_weight,
            vector_block,
        )
    )
    first = lax.all_gather(first_packed, ("dp", "seq"), axis=0, tiled=False)
    owners = first.shape[0]

    def owner_rows(matrix):
        return matrix.astype(jnp.bfloat16).reshape(owners, -1, D)

    def first_at(slot):
        return first[:, slot * shard_rows : (slot + 1) * shard_rows, :].reshape(D, D)

    full_query, full_key, full_value, full_cross_key, full_cross_value = (
        first_at(slot) for slot in range(5)
    )
    full_vectors = first[:, 5 * shard_rows :, :]
    packed = jnp.concatenate(
        (
            attn_out_weight,
            cross_query_weight,
            cross_out_weight,
            fc_in_blocks,
            fc_out_weight,
        )
    )
    packed, first = lax.optimization_barrier((packed, first))
    gathered = lax.all_gather(packed, ("dp", "seq"), axis=0, tiled=False)

    def square_at(slot):
        return gathered[:, slot * shard_rows : (slot + 1) * shard_rows, :].reshape(D, D)

    full_self_out, full_cross_query, full_cross_out = (square_at(slot) for slot in range(3))
    wide_start = 3 * shard_rows
    wide_stop = wide_start + wide_parts * shard_rows
    full_fc_in = jnp.transpose(
        gathered[:, wide_start:wide_stop, :].reshape(owners, wide_parts, shard_rows, D),
        (0, 2, 1, 3),
    ).reshape(D, wide_parts * D)
    out_stop = wide_stop + fc_out_weight.shape[0]
    full_fc_out = gathered[:, wide_stop:out_stop, :].reshape(wide_parts * D, D)

    def vector_at(slot):
        return full_vectors[:, slot, :shard_rows].reshape(D)

    (
        full_self_gain,
        full_self_shift,
        full_query_bias,
        full_value_bias,
        full_self_out_bias,
        full_cross_gain,
        full_cross_shift,
        full_cross_query_bias,
        full_cross_value_bias,
        full_cross_out_bias,
        full_mlp_gain,
        full_mlp_shift,
        full_fc_out_bias,
    ) = (vector_at(slot) for slot in range(13))
    full_fc_in_bias = full_vectors[:, 13, : fc_in_bias.shape[0]].reshape(-1)
    normed_self, scaled_self, inverse_self = norm_forward(
        input_rows, full_self_gain.astype(jnp.float32), full_self_shift.astype(jnp.float32)
    )
    normed_self_low = rounded(normed_self)
    query_rows = rounded(project(normed_self_low, full_query) + full_query_bias.astype(jnp.float32))
    key_rows = rounded(project(normed_self_low, full_key))
    value_rows = rounded(
        project(normed_self_low, full_value) + full_value_bias.astype(jnp.float32)
    )
    head_triple = lax.all_to_all(
        jnp.stack(
            tuple(to_pairs(rows, seq_count) for rows in (query_rows, key_rows, value_rows)), axis=1
        ),
        "seq",
        0,
        0,
    )
    head_queries, head_keys, head_values = (
        head_triple[:, slot].reshape(full_length, PAIR) for slot in range(3)
    )
    head_attended, head_log = self_forward(head_queries, head_keys, head_values, labels)
    attended_blocks = lax.all_to_all(
        rounded(head_attended).reshape(seq_count, local_len, PAIR), "seq", 0, 0
    )
    attended_self_low = from_pairs(attended_blocks)
    middle_rows = (
        input_rows
        + project(attended_self_low, full_self_out)
        + full_self_out_bias.astype(jnp.float32)
    )
    normed_cross, scaled_cross, inverse_cross = norm_forward(
        middle_rows, full_cross_gain.astype(jnp.float32), full_cross_shift.astype(jnp.float32)
    )
    normed_cross_low = rounded(normed_cross)
    cross_queries = rounded(
        project(normed_cross_low, full_cross_query) + full_cross_query_bias.astype(jnp.float32)
    )
    frame_count = memory.shape[0]
    frame_part = frame_count // seq_count
    frame_start = seq_index * frame_part
    memory_flat = memory.reshape(frame_count, D)
    memory_part = lax.dynamic_slice_in_dim(memory_flat, frame_start, frame_part, 0)
    memory_keys = rounded(project(memory_flat, full_cross_key))
    memory_values = rounded(
        project(memory_flat, full_cross_value) + full_cross_value_bias.astype(jnp.float32)
    )
    attended_cross_low, cross_log = cross_forward(
        memory_lengths, cross_queries, memory_keys, memory_values
    )
    after_rows = (
        middle_rows
        + project(attended_cross_low, full_cross_out)
        + full_cross_out_bias.astype(jnp.float32)
    )
    normed_mlp, scaled_mlp, inverse_mlp = norm_forward(
        after_rows, full_mlp_gain.astype(jnp.float32), full_mlp_shift.astype(jnp.float32)
    )
    normed_mlp_low = rounded(normed_mlp)
    hidden_pre = project(normed_mlp_low, full_fc_in) + full_fc_in_bias.astype(jnp.float32)
    activated, gelu_pull = jax.vjp(exact_gelu, hidden_pre)
    activated_low = rounded(activated)
    result_rows = (
        after_rows + project(activated_low, full_fc_out) + full_fc_out_bias.astype(jnp.float32)
    )
    output = rounded(result_rows).reshape(local_len, batch_count, D)
    back_fc_in, back_fc_out = full_fc_in, full_fc_out
    grad_result = out_grad.reshape(token_count, D)
    grad_mlp_low = rounded(grad_result)
    grad_fc_out_weight = weight_grad(activated_low, grad_mlp_low)
    grad_fc_out_bias = column_sums(grad_mlp_low)
    grad_activated = project_back(grad_mlp_low, back_fc_out)
    grad_hidden_low = rounded(gelu_pull(grad_activated)[0])
    grad_fc_in_blocks = tuple(
        weight_grad(normed_mlp_low, grad_hidden_low[:, part * D : (part + 1) * D])
        for part in range(wide_parts)
    )
    grad_fc_in_bias = column_sums(grad_hidden_low)
    grad_normed_mlp = project_back(grad_hidden_low, back_fc_in)
    grad_rows_mlp, grad_mlp_gain, grad_mlp_shift = norm_backward(
        grad_normed_mlp, scaled_mlp, inverse_mlp, full_mlp_gain.astype(jnp.float32)
    )
    grad_after = grad_result + grad_rows_mlp
    back_cross_query, back_cross_key, back_cross_value, back_cross_out = (
        full_cross_query,
        full_cross_key,
        full_cross_value,
        full_cross_out,
    )
    grad_cross_low = rounded(grad_after)
    grad_cross_out_weight = weight_grad(attended_cross_low, grad_cross_low)
    grad_cross_out_bias = column_sums(grad_cross_low)
    grad_attended_cross = rounded(project_back(grad_cross_low, back_cross_out))
    grad_cross_queries, grad_memory_kv = cross_backward(
        memory_lengths,
        cross_queries,
        memory_keys,
        memory_values,
        cross_log,
        grad_attended_cross,
    )
    dp_index = lax.axis_index("dp")
    core_bit, x_bit = dp_index % 2, dp_index // 2
    y_bit, low_bit, high_bit = seq_index % 2, (seq_index // 2) % 2, seq_index // 4
    memory_parts = grad_memory_kv.reshape(2, 2, 2, 2, frame_part, D)
    part_keys = halve(halve(memory_parts[0], 2, "seq", 1, y_bit), 1, "seq", 2, low_bit)
    part_values = halve(halve(memory_parts[1], 1, "seq", 2, low_bit), 1, "seq", 1, y_bit)
    part_flat_keys = halve(part_keys, 0, "seq", 4, high_bit)
    part_flat_values = halve(part_values, 0, "seq", 4, high_bit)
    part_memory_grad = (
        project_back(part_flat_keys, back_cross_key)
        + project_back(part_flat_values, back_cross_value)
    )
    grad_cross_key_weight = weight_grad(memory_part, part_flat_keys)
    grad_cross_value_weight = weight_grad(memory_part, part_flat_values)
    grad_cross_value_bias = column_sums(part_flat_values)
    grad_cross_query_weight = weight_grad(normed_cross_low, grad_cross_queries)
    grad_cross_query_bias = column_sums(grad_cross_queries)
    grad_normed_cross = project_back(grad_cross_queries, back_cross_query)
    grad_rows_cross, grad_cross_gain, grad_cross_shift = norm_backward(
        grad_normed_cross, scaled_cross, inverse_cross, full_cross_gain.astype(jnp.float32)
    )
    grad_middle = grad_after + grad_rows_cross
    back_query, back_key, back_value, back_self_out = (
        full_query,
        full_key,
        full_value,
        full_self_out,
    )
    grad_self_low = rounded(grad_middle)
    grad_attn_out_weight = weight_grad(attended_self_low, grad_self_low)
    grad_attn_out_bias = column_sums(grad_self_low)
    early_grads = jnp.concatenate(
        (
            *(owner_rows(block) for block in grad_fc_in_blocks),
            owner_rows(grad_fc_out_weight),
            owner_rows(grad_attn_out_weight),
            owner_rows(grad_cross_query_weight),
            owner_rows(grad_cross_out_weight),
        ),
        axis=1,
    )
    owned_early = lax.psum_scatter(
        early_grads, ("dp", "seq"), scatter_dimension=0, tiled=False
    )
    owned_early = owned_early.astype(jnp.float32)
    wide_rows = wide_parts * shard_rows
    owned_fc_in = jnp.transpose(
        owned_early[:wide_rows].reshape(wide_parts, shard_rows, D), (1, 0, 2)
    ).reshape(shard_rows, wide_parts * D)
    out_rows = wide_rows + fc_out_weight.shape[0]
    owned_fc_out = owned_early[wide_rows:out_rows]
    owned_middle = owned_early[out_rows:]
    grad_attended_self = rounded(project_back(grad_self_low, back_self_out))
    head_blocks = to_pairs(grad_attended_self, seq_count)
    head_grad = lax.all_to_all(head_blocks, "seq", 0, 0)
    head_grad = head_grad.reshape(full_length, PAIR)
    head_grads = self_backward(
        head_queries, head_keys, head_values, labels, head_attended, head_log, head_grad
    )
    grad_blocks = jnp.stack(
        tuple(part.reshape(seq_count, local_len, PAIR) for part in head_grads), axis=1
    )
    grad_triple = lax.all_to_all(grad_blocks, "seq", 0, 0)
    grad_query_low, grad_key_low, grad_value_low = (
        from_pairs(grad_triple[:, slot]) for slot in range(3)
    )
    grad_query_weight = weight_grad(normed_self_low, grad_query_low)
    grad_query_bias = column_sums(grad_query_low)
    grad_key_weight = weight_grad(normed_self_low, grad_key_low)
    grad_value_weight = weight_grad(normed_self_low, grad_value_low)
    grad_value_bias = column_sums(grad_value_low)
    grad_normed_self = (
        project_back(grad_query_low, back_query)
        + project_back(grad_key_low, back_key)
        + project_back(grad_value_low, back_value)
    )
    grad_rows_self, grad_self_gain, grad_self_shift = norm_backward(
        grad_normed_self, scaled_self, inverse_self, full_self_gain.astype(jnp.float32)
    )
    token_grad = (grad_middle + grad_rows_self).reshape(local_len, batch_count, D)
    late_block = place_rows(
        tuple(
            vector.reshape(owners, -1)
            for vector in (
                grad_self_gain,
                grad_self_shift,
                grad_query_bias,
                grad_value_bias,
                grad_attn_out_bias,
                grad_cross_gain,
                grad_cross_shift,
                grad_cross_query_bias,
                grad_cross_value_bias,
                grad_cross_out_bias,
                grad_mlp_gain,
                grad_mlp_shift,
                grad_fc_out_bias,
                grad_fc_in_bias,
            )
        ),
        16,
    )
    late_grads = jnp.concatenate(
        (
            owner_rows(grad_query_weight),
            owner_rows(grad_key_weight),
            owner_rows(grad_value_weight),
            owner_rows(grad_cross_key_weight),
            owner_rows(grad_cross_value_weight),
            late_block,
        ),
        axis=1,
    )
    late_rows = late_grads.shape[1]
    by_core = halve(late_grads.reshape(2, 2, 2, 2, 2, late_rows, D), 1, "dp", 1, core_bit)
    cut_row = late_rows // 16 * 8
    upper = by_core[:, :, :, :, :cut_row]
    lower = by_core[:, :, :, :, cut_row:]
    upper = halve(halve(upper, 0, "dp", 2, x_bit), 2, "seq", 1, y_bit)
    lower = halve(halve(lower, 3, "seq", 1, y_bit), 0, "dp", 2, x_bit)
    by_column = jnp.concatenate((upper, lower), axis=2)
    owned_late = halve(
        halve(by_column, 1, "seq", 2, low_bit), 0, "seq", 4, high_bit, jnp.float32
    )
    memory_grad = lax.all_gather(part_memory_grad.astype(jnp.bfloat16), "seq", axis=0, tiled=True)
    memory_grad = widen_frames(memory_grad)
    owned_vectors = owned_late[5 * shard_rows :]

    def own_square(slot):
        return owned_late[slot * shard_rows : (slot + 1) * shard_rows]

    def own_middle(slot):
        return owned_middle[slot * shard_rows : (slot + 1) * shard_rows]

    def own_vector(slot):
        return owned_vectors[slot, :shard_rows]

    owned_fc_in_bias = owned_vectors[13, : fc_in_bias.shape[0]]
    return (
        output,
        token_grad,
        memory_grad,
        own_vector(0),
        own_vector(1),
        own_square(0),
        own_vector(2),
        own_square(1),
        own_square(2),
        own_vector(3),
        own_middle(0),
        own_vector(4),
        own_vector(5),
        own_vector(6),
        own_middle(1),
        own_vector(7),
        own_square(3),
        own_square(4),
        own_vector(8),
        own_middle(2),
        own_vector(9),
        own_vector(10),
        own_vector(11),
        owned_fc_in,
        owned_fc_in_bias,
        owned_fc_out,
        own_vector(12),
    )


def local(
    tokens,
    memory,
    piece_starts,
    memory_lengths,
    self_gain,
    self_shift,
    query_weight,
    query_bias,
    key_weight,
    value_weight,
    value_bias,
    attn_out_weight,
    attn_out_bias,
    cross_gain,
    cross_shift,
    cross_query_weight,
    cross_query_bias,
    cross_key_weight,
    cross_value_weight,
    cross_value_bias,
    cross_out_weight,
    cross_out_bias,
    mlp_gain,
    mlp_shift,
    fc_in_weight,
    fc_in_bias,
    fc_out_weight,
    fc_out_bias,
    out_grad,
):
    local_len, batch_count, _ = tokens.shape
    seq_count = lax.axis_size("seq")
    seq_index = lax.axis_index("seq")
    full_length = local_len * seq_count
    token_count = local_len * batch_count
    query_pos = seq_index * local_len + jnp.arange(local_len, dtype=jnp.int32)
    query_label = piece_labels(query_pos, piece_starts)
    input_rows = tokens.reshape(token_count, D).astype(jnp.float32)
    shard_rows = query_weight.shape[0]
    wide_parts = fc_in_weight.shape[1] // D
    vectors = jnp.concatenate(
        (
            self_gain,
            self_shift,
            query_bias,
            value_bias,
            attn_out_bias,
            cross_gain,
            cross_shift,
            cross_query_bias,
            cross_value_bias,
            cross_out_bias,
            mlp_gain,
            mlp_shift,
            fc_out_bias,
            fc_in_bias,
        )
    )
    vector_rows = 8
    vector_block = jnp.pad(vectors, (0, vector_rows * D - vectors.shape[0])).reshape(vector_rows, D)
    fc_in_blocks = jnp.transpose(
        fc_in_weight.reshape(shard_rows, wide_parts, D), (1, 0, 2)
    ).reshape(wide_parts * shard_rows, D)
    packed = jnp.concatenate(
        (
            query_weight,
            key_weight,
            value_weight,
            attn_out_weight,
            cross_query_weight,
            cross_key_weight,
            cross_value_weight,
            cross_out_weight,
            fc_in_blocks,
            fc_out_weight,
            vector_block,
        )
    )
    gathered = lax.all_gather(packed, ("dp", "seq"), axis=0, tiled=False)
    owners = gathered.shape[0]

    def square_at(slot):
        return gathered[:, slot * shard_rows : (slot + 1) * shard_rows, :].reshape(D, D)

    full_query, full_key, full_value, full_self_out = (square_at(slot) for slot in range(4))
    full_cross_query, full_cross_key, full_cross_value, full_cross_out = (
        square_at(slot) for slot in range(4, 8)
    )
    wide_start = 8 * shard_rows
    wide_stop = wide_start + wide_parts * shard_rows
    full_fc_in = jnp.transpose(
        gathered[:, wide_start:wide_stop, :].reshape(owners, wide_parts, shard_rows, D),
        (0, 2, 1, 3),
    ).reshape(D, wide_parts * D)
    out_stop = wide_stop + fc_out_weight.shape[0]
    full_fc_out = gathered[:, wide_stop:out_stop, :].reshape(wide_parts * D, D)
    full_vectors = gathered[:, out_stop:, :].reshape(owners, vector_rows * D)

    def vector_at(slot):
        return full_vectors[:, slot * shard_rows : (slot + 1) * shard_rows].reshape(D)

    (
        full_self_gain,
        full_self_shift,
        full_query_bias,
        full_value_bias,
        full_self_out_bias,
        full_cross_gain,
        full_cross_shift,
        full_cross_query_bias,
        full_cross_value_bias,
        full_cross_out_bias,
        full_mlp_gain,
        full_mlp_shift,
        full_fc_out_bias,
    ) = (vector_at(slot) for slot in range(13))
    full_fc_in_bias = full_vectors[
        :, 13 * shard_rows : 13 * shard_rows + fc_in_bias.shape[0]
    ].reshape(-1)
    normed_self, scaled_self, inverse_self = norm_forward(
        input_rows, full_self_gain.astype(jnp.float32), full_self_shift.astype(jnp.float32)
    )
    normed_self_low = rounded(normed_self)
    query_rows = rounded(project(normed_self_low, full_query) + full_query_bias.astype(jnp.float32))
    key_rows = rounded(project(normed_self_low, full_key)).reshape(local_len, batch_count, D)
    value_rows = rounded(
        project(normed_self_low, full_value) + full_value_bias.astype(jnp.float32)
    ).reshape(local_len, batch_count, D)
    query_heads = query_rows.reshape(local_len, batch_count, HEADS, HEAD)

    def key_block_scores(key_block, key_pos):
        key_heads = key_block.reshape(key_block.shape[0], batch_count, HEADS, HEAD)
        raw_scores = jnp.einsum(
            "qbhd,kbhd->qbhk", query_heads, key_heads, preferred_element_type=jnp.float32
        )
        allowed = visible(query_pos, query_label, key_pos, piece_labels(key_pos, piece_starts))
        return (raw_scores * 0.125, allowed)

    start_state = (
        jnp.full((local_len, batch_count, HEADS), neg_large, jnp.float32),
        jnp.zeros((local_len, batch_count, HEADS), jnp.float32),
        jnp.zeros((local_len, batch_count, HEADS, HEAD), jnp.float32),
    )
    running = start_state
    kv_piece = lax.all_gather(
        jnp.concatenate((key_rows, value_rows), axis=2), "seq", axis=0, tiled=True
    )
    key_piece = kv_piece[:, :, :D]
    value_piece = kv_piece[:, :, D:]
    block_rows = math.gcd(key_piece.shape[0], 512)

    def fold_block(inner_state, block_index):
        row_max, row_total, weighted_sum = inner_state
        block_start = block_index * block_rows
        key_block = lax.dynamic_slice_in_dim(key_piece, block_start, block_rows, 0)
        value_block = lax.dynamic_slice_in_dim(value_piece, block_start, block_rows, 0).reshape(
            block_rows, batch_count, HEADS, HEAD
        )
        key_pos = block_start + jnp.arange(block_rows, dtype=jnp.int32)
        scores, allowed = key_block_scores(key_block, key_pos)
        new_max = jnp.maximum(row_max, jnp.max(jnp.where(allowed, scores, neg_large), axis=-1))
        exp_terms = jnp.where(allowed, jnp.exp(scores - new_max[..., None]), 0.0)
        factor = jnp.exp(row_max - new_max)
        row_total = row_total * factor + jnp.sum(exp_terms, axis=-1)
        weighted_sum = weighted_sum * factor[..., None] + jnp.einsum(
            "qbhk,kbhd->qbhd", rounded(exp_terms), value_block, preferred_element_type=jnp.float32
        )
        return ((new_max, row_total, weighted_sum), None)

    running, unused = lax.scan(
        fold_block, running, jnp.arange(key_piece.shape[0] // block_rows, dtype=jnp.int32)
    )
    row_max, row_total, weighted_sum = running
    attended_self = weighted_sum / row_total[..., None]
    log_total = row_max + jnp.log(row_total)
    attended_self_low = rounded(attended_self.reshape(token_count, D))
    middle_rows = (
        input_rows
        + project(attended_self_low, full_self_out)
        + full_self_out_bias.astype(jnp.float32)
    )
    normed_cross, scaled_cross, inverse_cross = norm_forward(
        middle_rows, full_cross_gain.astype(jnp.float32), full_cross_shift.astype(jnp.float32)
    )
    normed_cross_low = rounded(normed_cross)
    cross_queries = rounded(
        project(normed_cross_low, full_cross_query) + full_cross_query_bias.astype(jnp.float32)
    ).reshape(local_len, batch_count, HEADS, HEAD)
    frame_count = memory.shape[0]
    frame_part = frame_count // seq_count
    frame_start = seq_index * frame_part
    memory_part = lax.dynamic_slice_in_dim(memory, frame_start, frame_part, 0).reshape(
        frame_part * batch_count, D
    )
    memory_flat = memory.reshape(frame_count * batch_count, D)
    memory_keys = rounded(project(memory_flat, full_cross_key)).reshape(frame_count, batch_count, D)
    memory_values = rounded(
        project(memory_flat, full_cross_value) + full_cross_value_bias.astype(jnp.float32)
    ).reshape(frame_count, batch_count, D)
    memory_key_heads = memory_keys.reshape(frame_count, batch_count, HEADS, HEAD)
    memory_value_heads = memory_values.reshape(frame_count, batch_count, HEADS, HEAD)
    frame_valid = (jnp.arange(frame_count, dtype=jnp.int32)[None, :] < memory_lengths[:, None])[
        None, :, None, :
    ]
    cross_scores = (
        jnp.einsum(
            "qbhd,kbhd->qbhk", cross_queries, memory_key_heads, preferred_element_type=jnp.float32
        )
        * 0.125
    )
    cross_max = jnp.max(jnp.where(frame_valid, cross_scores, neg_large), axis=-1, keepdims=True)
    cross_exp = jnp.where(frame_valid, jnp.exp(cross_scores - cross_max), 0.0)
    cross_probs = cross_exp / jnp.sum(cross_exp, axis=-1, keepdims=True)
    cross_probs_low = rounded(cross_probs)
    attended_cross = jnp.einsum(
        "qbhk,kbhd->qbhd", cross_probs_low, memory_value_heads, preferred_element_type=jnp.float32
    )
    attended_cross_low = rounded(attended_cross.reshape(token_count, D))
    after_rows = (
        middle_rows
        + project(attended_cross_low, full_cross_out)
        + full_cross_out_bias.astype(jnp.float32)
    )
    normed_mlp, scaled_mlp, inverse_mlp = norm_forward(
        after_rows, full_mlp_gain.astype(jnp.float32), full_mlp_shift.astype(jnp.float32)
    )
    normed_mlp_low = rounded(normed_mlp)
    hidden_pre = project(normed_mlp_low, full_fc_in) + full_fc_in_bias.astype(jnp.float32)
    activated, gelu_pull = jax.vjp(exact_gelu, hidden_pre)
    activated_low = rounded(activated)
    result_rows = (
        after_rows + project(activated_low, full_fc_out) + full_fc_out_bias.astype(jnp.float32)
    )
    output = rounded(result_rows).reshape(local_len, batch_count, D)
    back_fc_in, back_fc_out = full_fc_in, full_fc_out
    grad_result = out_grad.reshape(token_count, D)
    grad_mlp_low = rounded(grad_result)
    grad_fc_out_weight = weight_grad(activated_low, grad_mlp_low)
    grad_fc_out_bias = column_sums(grad_mlp_low)
    grad_activated = project_back(grad_mlp_low, back_fc_out)
    grad_hidden_low = rounded(gelu_pull(grad_activated)[0])
    grad_fc_in_weight = weight_grad(normed_mlp_low, grad_hidden_low)
    grad_fc_in_bias = column_sums(grad_hidden_low)
    grad_normed_mlp = project_back(grad_hidden_low, back_fc_in)
    grad_rows_mlp, grad_mlp_gain, grad_mlp_shift = norm_backward(
        grad_normed_mlp, scaled_mlp, inverse_mlp, full_mlp_gain.astype(jnp.float32)
    )
    early_grads = jnp.concatenate(
        (
            jnp.transpose(
                grad_fc_in_weight.astype(jnp.bfloat16).reshape(
                    owners, shard_rows, wide_parts, D
                ),
                (0, 2, 1, 3),
            ).reshape(owners, wide_parts * shard_rows, D),
            grad_fc_out_weight.astype(jnp.bfloat16).reshape(owners, -1, D),
        ),
        axis=1,
    )
    owned_early = lax.psum_scatter(
        early_grads, ("dp", "seq"), scatter_dimension=0, tiled=False
    ).astype(jnp.float32)
    wide_rows = wide_parts * shard_rows
    owned_fc_in = jnp.transpose(
        owned_early[:wide_rows].reshape(wide_parts, shard_rows, D), (1, 0, 2)
    ).reshape(shard_rows, wide_parts * D)
    owned_fc_out = owned_early[wide_rows:]
    grad_after = grad_result + grad_rows_mlp
    back_cross_query, back_cross_key, back_cross_value, back_cross_out = (
        full_cross_query,
        full_cross_key,
        full_cross_value,
        full_cross_out,
    )
    grad_cross_low = rounded(grad_after)
    grad_cross_out_weight = weight_grad(attended_cross_low, grad_cross_low)
    grad_cross_out_bias = column_sums(grad_cross_low)
    grad_attended_cross = rounded(project_back(grad_cross_low, back_cross_out)).reshape(
        local_len, batch_count, HEADS, HEAD
    )
    grad_cross_probs = jnp.einsum(
        "qbhd,kbhd->qbhk",
        grad_attended_cross,
        memory_value_heads,
        preferred_element_type=jnp.float32,
    )
    cross_delta = jnp.sum(cross_probs * grad_cross_probs, axis=-1, keepdims=True)
    grad_cross_scores = rounded(cross_probs * (grad_cross_probs - cross_delta) * 0.125)
    grad_cross_queries = rounded(
        jnp.einsum(
            "qbhk,kbhd->qbhd",
            grad_cross_scores,
            memory_key_heads,
            preferred_element_type=jnp.float32,
        ).reshape(token_count, D)
    )
    grad_memory_keys = jnp.einsum(
        "qbhk,qbhd->kbhd", grad_cross_scores, cross_queries, preferred_element_type=jnp.float32
    ).reshape(frame_count, batch_count, D)
    grad_memory_values = jnp.einsum(
        "qbhk,qbhd->kbhd", cross_probs_low, grad_attended_cross, preferred_element_type=jnp.float32
    ).reshape(frame_count, batch_count, D)
    grad_memory_kv = jnp.concatenate((grad_memory_keys, grad_memory_values), axis=2)
    grad_cross_query_weight = weight_grad(normed_cross_low, grad_cross_queries)
    grad_cross_query_bias = column_sums(grad_cross_queries)
    grad_normed_cross = project_back(grad_cross_queries, back_cross_query)
    grad_rows_cross, grad_cross_gain, grad_cross_shift = norm_backward(
        grad_normed_cross, scaled_cross, inverse_cross, full_cross_gain.astype(jnp.float32)
    )
    grad_middle = grad_after + grad_rows_cross
    back_query, back_key, back_value, back_self_out = (
        full_query,
        full_key,
        full_value,
        full_self_out,
    )
    grad_self_low = rounded(grad_middle)
    grad_attn_out_weight = weight_grad(attended_self_low, grad_self_low)
    grad_attn_out_bias = column_sums(grad_self_low)
    grad_attended_self = rounded(project_back(grad_self_low, back_self_out)).reshape(
        local_len, batch_count, HEADS, HEAD
    )
    self_delta = jnp.sum(grad_attended_self.astype(jnp.float32) * attended_self, axis=-1)

    def score_grads(key_block, value_block, key_pos):
        scores, allowed = key_block_scores(key_block, key_pos)
        attn_probs = jnp.where(allowed, jnp.exp(scores - log_total[..., None]), 0.0)
        grad_probs = jnp.einsum(
            "qbhd,kbhd->qbhk", grad_attended_self, value_block, preferred_element_type=jnp.float32
        )
        grad_scores = rounded(attn_probs * (grad_probs - self_delta[..., None]) * 0.125)
        return (grad_scores, attn_probs)

    zero_query_grad = jnp.zeros((local_len, batch_count, HEADS, HEAD), jnp.float32)
    back_state = (zero_query_grad, jnp.zeros((full_length, batch_count, 2 * D), jnp.float32))
    running = back_state
    self_key_piece = key_piece
    self_value_piece = value_piece
    self_block_rows = math.gcd(self_key_piece.shape[0], 512)

    def back_block(inner_state, block_index):
        grad_query_sum, kv_grads = inner_state
        block_start = block_index * self_block_rows
        key_block = lax.dynamic_slice_in_dim(self_key_piece, block_start, self_block_rows, 0)
        value_block = lax.dynamic_slice_in_dim(
            self_value_piece, block_start, self_block_rows, 0
        ).reshape(self_block_rows, batch_count, HEADS, HEAD)
        key_pos = block_start + jnp.arange(self_block_rows, dtype=jnp.int32)
        grad_scores, attn_probs = score_grads(key_block, value_block, key_pos)
        key_heads = key_block.reshape(self_block_rows, batch_count, HEADS, HEAD)
        grad_query_sum = grad_query_sum + jnp.einsum(
            "qbhk,kbhd->qbhd", grad_scores, key_heads, preferred_element_type=jnp.float32
        )
        grad_key_block = jnp.einsum(
            "qbhk,qbhd->kbhd", grad_scores, query_heads, preferred_element_type=jnp.float32
        ).reshape(self_block_rows, batch_count, D)
        grad_value_block = jnp.einsum(
            "qbhk,qbhd->kbhd",
            rounded(attn_probs),
            grad_attended_self,
            preferred_element_type=jnp.float32,
        ).reshape(self_block_rows, batch_count, D)
        kv_grads = lax.dynamic_update_slice_in_dim(
            kv_grads, jnp.concatenate((grad_key_block, grad_value_block), axis=2), block_start, 0
        )
        return ((grad_query_sum, kv_grads), None)

    running, unused = lax.scan(
        back_block, running, jnp.arange(self_key_piece.shape[0] // self_block_rows, dtype=jnp.int32)
    )
    grad_query_sum = running[0]
    joint_kv = jnp.concatenate(
        (
            running[1].astype(jnp.bfloat16).reshape(seq_count, local_len, batch_count, 2 * D),
            grad_memory_kv.astype(jnp.bfloat16).reshape(
                seq_count, frame_part, batch_count, 2 * D
            ),
        ),
        axis=1,
    )
    own_joint = lax.psum_scatter(joint_kv, "seq", scatter_dimension=0, tiled=False)
    own_kv = own_joint[:local_len]
    part_kv = own_joint[local_len:]
    grad_key_low = own_kv[:, :, :D].reshape(token_count, D)
    grad_value_low = own_kv[:, :, D:].reshape(token_count, D)
    part_flat_keys = part_kv[:, :, :D].reshape(frame_part * batch_count, D)
    part_flat_values = part_kv[:, :, D:].reshape(frame_part * batch_count, D)
    part_memory_grad = (
        project_back(part_flat_keys, back_cross_key)
        + project_back(part_flat_values, back_cross_value)
    ).reshape(frame_part, batch_count, D)
    grad_cross_key_weight = weight_grad(memory_part, part_flat_keys)
    grad_cross_value_weight = weight_grad(memory_part, part_flat_values)
    grad_cross_value_bias = column_sums(part_flat_values)
    grad_query_low = rounded(grad_query_sum.reshape(token_count, D))
    grad_query_weight = weight_grad(normed_self_low, grad_query_low)
    grad_query_bias = column_sums(grad_query_low)
    grad_key_weight = weight_grad(normed_self_low, grad_key_low)
    grad_value_weight = weight_grad(normed_self_low, grad_value_low)
    grad_value_bias = column_sums(grad_value_low)
    grad_normed_self = (
        project_back(grad_query_low, back_query)
        + project_back(grad_key_low, back_key)
        + project_back(grad_value_low, back_value)
    )
    grad_rows_self, grad_self_gain, grad_self_shift = norm_backward(
        grad_normed_self, scaled_self, inverse_self, full_self_gain.astype(jnp.float32)
    )
    token_grad = (grad_middle + grad_rows_self).reshape(local_len, batch_count, D)

    def owner_rows(matrix):
        return matrix.astype(jnp.bfloat16).reshape(owners, -1, D)

    late_vectors = jnp.concatenate(
        tuple(
            vector.reshape(owners, -1)
            for vector in (
                grad_self_gain,
                grad_self_shift,
                grad_query_bias,
                grad_value_bias,
                grad_attn_out_bias,
                grad_cross_gain,
                grad_cross_shift,
                grad_cross_query_bias,
                grad_cross_value_bias,
                grad_cross_out_bias,
                grad_mlp_gain,
                grad_mlp_shift,
                grad_fc_out_bias,
                grad_fc_in_bias,
            )
        ),
        axis=1,
    )
    late_block = jnp.pad(
        late_vectors.astype(jnp.bfloat16),
        ((0, 0), (0, vector_rows * D - late_vectors.shape[1])),
    ).reshape(owners, vector_rows, D)
    late_grads = jnp.concatenate(
        (
            owner_rows(grad_query_weight),
            owner_rows(grad_key_weight),
            owner_rows(grad_value_weight),
            owner_rows(grad_attn_out_weight),
            owner_rows(grad_cross_query_weight),
            owner_rows(grad_cross_key_weight),
            owner_rows(grad_cross_value_weight),
            owner_rows(grad_cross_out_weight),
            late_block,
        ),
        axis=1,
    )
    owned_late = lax.psum_scatter(
        late_grads, ("dp", "seq"), scatter_dimension=0, tiled=False
    ).astype(jnp.float32)
    memory_grad = lax.all_gather(
        part_memory_grad.astype(jnp.bfloat16), "seq", axis=0, tiled=True
    ).astype(jnp.float32)
    owned_vectors = owned_late[8 * shard_rows :].reshape(-1)

    def own_square(slot):
        return owned_late[slot * shard_rows : (slot + 1) * shard_rows]

    def own_vector(slot):
        return owned_vectors[slot * shard_rows : (slot + 1) * shard_rows]

    owned_fc_in_bias = owned_vectors[13 * shard_rows : 13 * shard_rows + fc_in_bias.shape[0]]
    return (
        output,
        token_grad,
        memory_grad,
        own_vector(0),
        own_vector(1),
        own_square(0),
        own_vector(2),
        own_square(1),
        own_square(2),
        own_vector(3),
        own_square(3),
        own_vector(4),
        own_vector(5),
        own_vector(6),
        own_square(4),
        own_vector(7),
        own_square(5),
        own_square(6),
        own_vector(8),
        own_square(7),
        own_vector(9),
        own_vector(10),
        own_vector(11),
        owned_fc_in,
        owned_fc_in_bias,
        owned_fc_out,
        own_vector(12),
    )


def solution(mesh):
    in_specs = (
        P("seq", "dp", None),
        P(None, "dp", None),
        P("dp", None),
        P("dp"),
        P(("dp", "seq")),
        P(("dp", "seq")),
        P(("dp", "seq"), None),
        P(("dp", "seq")),
        P(("dp", "seq"), None),
        P(("dp", "seq"), None),
        P(("dp", "seq")),
        P(("dp", "seq"), None),
        P(("dp", "seq")),
        P(("dp", "seq")),
        P(("dp", "seq")),
        P(("dp", "seq"), None),
        P(("dp", "seq")),
        P(("dp", "seq"), None),
        P(("dp", "seq"), None),
        P(("dp", "seq")),
        P(("dp", "seq"), None),
        P(("dp", "seq")),
        P(("dp", "seq")),
        P(("dp", "seq")),
        P(("dp", "seq"), None),
        P(("dp", "seq")),
        P(("dp", "seq"), None),
        P(("dp", "seq")),
        P("seq", "dp", None),
    )
    out_specs = (
        P("seq", "dp", None),
        P("seq", "dp", None),
        P(None, "dp", None),
        P(("dp", "seq")),
        P(("dp", "seq")),
        P(("dp", "seq"), None),
        P(("dp", "seq")),
        P(("dp", "seq"), None),
        P(("dp", "seq"), None),
        P(("dp", "seq")),
        P(("dp", "seq"), None),
        P(("dp", "seq")),
        P(("dp", "seq")),
        P(("dp", "seq")),
        P(("dp", "seq"), None),
        P(("dp", "seq")),
        P(("dp", "seq"), None),
        P(("dp", "seq"), None),
        P(("dp", "seq")),
        P(("dp", "seq"), None),
        P(("dp", "seq")),
        P(("dp", "seq")),
        P(("dp", "seq")),
        P(("dp", "seq"), None),
        P(("dp", "seq")),
        P(("dp", "seq"), None),
        P(("dp", "seq")),
    )
    by_heads = mesh.shape["dp"] == 4 and mesh.shape["seq"] == 8

    def layer(*arrays):
        return local_heads(*arrays)

    return jax.shard_map(
        layer if by_heads else local,
        mesh=mesh,
        in_specs=in_specs,
        out_specs=out_specs,
        check_vma=False,
    )
```

profile of v0, /device:TPU:0, one launch (start us, length us, event | category | flops | bytes accessed | tf_op | source)
XLA Modules:
  0.0 666.6 jit_solution(10586546698974052011)
XLA Ops:
  25.7 69.2 %all-gather.8.cloned.1.call-done = bf16[4352,768]{1,0:T(8,128)(2,1)} async-done(((bf16[136,768]{1,0:T(8,128)(2,1)}), bf16[4352,768]{1,0:T(8,128)(2,1)}) %all-gather.8.cloned.1.call-update) | async-done | bytes 6684688 | tf_op jit(solution)/shard_map/all_gather | solution.py:507
  95.3 2.7 fusion.86
  99.0 5.0 fusion.87
  105.9 2.6 fusion.19
  109.7 2.6 convolution_convert_fusion.16
  112.3 1.9 copy.237
  116.7 4.4 all-to-all-start
  135.8 40.6 %all-to-all-done = bf16[8,3,256,128]{2,3,1,0:T(8,128)(2,1)} async-done(((bf16[8,3,256,128]{2,3,1,0:T(8,128)(2,1)}), bf16[8,3,256,128]{2,3,1,0:T(8,128)(2,1)}, u32[]{:S(2)}, u32[]{:S(2)}) %all-to-all-start) | async-done | bytes 1572896 | tf_op jit(solution)/shard_map/all_to_all | solution.py:573
  176.4 2.5 fusion.90
  178.8 2.0 copy.243
  180.9 2.1 copy.242
  183.9 23.0 %self_forward.1 = (f32[2048,128]{1,0:T(8,128)}, f32[2048,128]{1,0:T(8,128)}) custom-call(bf16[2048,128]{1,0:T(8,128)(2,1)} %bitcast.377, bf16[2048,128]{1,0:T(8,128)(2,1)} %bitcast.375, bf16[2048,128]{1,0:T(8,128)(2,1)} %bitcast.373, s32[2048,1]{1,0:T(8,128)} %copy.244.column_ref, s32[1,2048]{1,0:T(1,128)} %bitcast.426), custom_call_target="tpu_custom_call" | custom-call | tf_op jit(solution)/shard_map/self_forward/pallas_call | solution.py:187
  209.4 3.6 all-to-all-start.1
  213.3 4.9 fusion.7.key_ref
  218.2 3.5 fusion.8.value_ref
  221.6 6.2 all-to-all-done.1
  228.6 3.6 fusion.85
  232.2 7.0 %fusion.84 = (bf16[32,96,768]{2,1,0:T(8,128)(2,1)}, bf16[32,96,768]{2,1,0:T(8,128)(2,1)S(1)}) fusion(bf16[32,264,768]{2,1,0:T(8,128)(2,1)} %bitcast.353), kind=kLoop, calls=%fused_computation.258 | loop fusion | bytes 18874368 | tf_op jit(solution)/shard_map/slice | solution.py:543
  239.2 2.3 copy.257
  241.6 3.3 copy.312
  247.5 11.7 %cross_forward.1 = (bf16[256,768]{1,0:T(8,128)(2,1)}, f32[256,768]{1,0:T(8,128)}) custom-call(s32[1]{0:T(128)S(6)} %copy.366.length_ref, bf16[256,768]{1,0:T(8,128)(2,1)} %fusion.21.query_ref, bf16[1536,768]{1,0:T(8,128)(2,1)} %fusion.7.key_ref, bf16[1536,768]{1,0:T(8,128)(2,1)} %fusion.8.value_ref), custom_call_target="tpu_custom_call" | custom-call | tf_op jit(solution)/shard_map/cross_forward/pallas_call | solution.py:368
  259.2 2.0 fusion.93
  261.7 10.9 %multiply_convert_fusion = (bf16[256,3072]{1,0:T(8,128)(2,1)}, f32[256,3072]{1,0:T(8,128)S(1)}, f32[256,3072]{1,0:T(8,128)S(1)}) fusion(f32[3072]{0:T(1024)S(1)} %copy-done.78, bf16[256,768]{1,0:T(8,128)(2,1)S(1)} %add_convert_fusion.2, bf16[768,3072]{1,0:T(8,128)(2,1)} %bitcast.381), kind=kOutput, calls=%fused_computation.11 | convolution fusion | flops 1259864064 | bytes 12988416 | tf_op jit(solution)/shard_map/dot_general | solution.py:26
  272.6 2.8 fusion.94
  275.3 2.1 multiply_reduce_fusion.1
  280.6 21.1 %cross_backward.1 = (bf16[256,768]{1,0:T(8,128)(2,1)}, bf16[2,1536,768]{2,1,0:T(8,128)(2,1)}) custom-call(s32[1]{0:T(128)S(6)} %copy.366.length_ref, bf16[256,768]{1,0:T(8,128)(2,1)} %fusion.21.query_ref, bf16[1536,768]{1,0:T(8,128)(2,1)} %fusion.7.key_ref, bf16[1536,768]{1,0:T(8,128)(2,1)} %fusion.8.value_ref, f32[256,768]{1,0:T(8,128)} %get-tuple-element.40.log_ref, ...), custom_call_target="tpu_custom_call" | custom-call | tf_op jit(solution)/shard_map/cross_backward/pallas_call | solution.py:411
  301.7 4.1 fusion.88
  309.0 2.4 dynamic-slice_bitcast_fusion.2
  312.1 23.0 %collective-permute-done.3 = bf16[2,2,192,768]{3,2,1,0:T(8,128)(2,1)} collective-permute-done((bf16[2,2,192,768]{3,2,1,0:T(8,128)(2,1)}, bf16[2,2,192,768]{3,2,1,0:T(8,128)(2,1)}, u32[]{:S(2)}, u32[]{:S(2)}) %collective-permute-start.3) | collective-permute-done | bytes 1179680 | tf_op jit(solution)/shard_map/ppermute | solution.py:339
  335.1 1.9 fusion.9
  337.1 1.9 collective-permute-start.4
  341.7 2.6 convolution_convert_fusion.7
  344.2 6.5 collective-permute-done.4
  351.0 2.4 collective-permute-start.5
  353.4 2.7 collective-permute-done.1
  356.3 2.2 collective-permute-start.2
  358.5 15.2 %collective-permute-done.5 = bf16[192,768]{1,0:T(8,128)(2,1)S(1)} collective-permute-done((bf16[192,768]{1,0:T(8,128)(2,1)S(1)}, bf16[192,768]{1,0:T(8,128)(2,1)S(1)}, u32[]{:S(2)}, u32[]{:S(2)}) %collective-permute-start.5) | collective-permute-done | bytes 294944 | tf_op jit(solution)/shard_map/ppermute | solution.py:339
  375.0 3.1 collective-permute-done.2
  390.3 2.4 constant_dynamic-update-slice_fusion.14
  400.0 1.8 convolution_convert_fusion.14
  403.7 34.8 %all_to_all.20 = bf16[8,256,128]{1,2,0:T(8,128)(2,1)} all-to-all(bf16[8,256,128]{1,2,0:T(8,128)(2,1)S(1)} %pad.118), channel_id=1, replica_groups=mesh['dp'=4,'seq'=8] {'seq'}, dimensions={0} | all-to-all | bytes 1048576 | tf_op jit(solution)/shard_map/all_to_all | solution.py:718
  438.5 2.0 copy.260
  440.6 26.1 %self_backward.1 = (bf16[2048,128]{1,0:T(8,128)(2,1)}, bf16[2048,128]{1,0:T(8,128)(2,1)}, bf16[2048,128]{1,0:T(8,128)(2,1)}) custom-call(bf16[2048,128]{1,0:T(8,128)(2,1)} %bitcast.378, bf16[2048,128]{1,0:T(8,128)(2,1)} %bitcast.376, bf16[2048,128]{1,0:T(8,128)(2,1)} %bitcast.374, s32[2048,1]{1,0:T(8,128)} %copy.244.column_ref, s32[1,2048]{1,0:T(1,128)} %bitcast.427, ...), custom_call_target="tpu_custom_call" | custom-call | tf_op jit(solution)/shard_map/self_backward/pallas_call | solution.py:279
  466.7 2.1 copy.262
  468.8 2.2 copy.263
  471.0 2.1 copy.264
  473.0 2.8 pad_maximum_fusion.1
  475.9 4.7 all-to-all-start.3
  499.6 2.6 convolution_convert_fusion.10
  502.2 38.4 %all-to-all-done.3 = bf16[8,3,256,128]{2,3,1,0:T(8,128)(2,1)} async-done(((bf16[8,3,256,128]{2,3,1,0:T(8,128)(2,1)}), bf16[8,3,256,128]{2,3,1,0:T(8,128)(2,1)}, u32[]{:S(2)}, u32[]{:S(2)}) %all-to-all-start.3) | async-done | bytes 1572896 | tf_op jit(solution)/shard_map/all_to_all | solution.py:726
  540.6 2.0 bitcast_reduce_fusion.1
  546.2 2.1 fusion.39
  573.5 4.4 select_dynamic-update-slice_fusion
  577.9 2.0 dynamic-slice_bitcast_fusion
  580.0 1.7 copy-done.11
  581.7 6.3 collective-permute-done.6
  588.0 4.2 fusion
  599.0 17.5 %collective-permute-done.7 = bf16[2,2,2,64,768]{4,3,0,1,2:T(8,128)(2,1)} collective-permute-done((bf16[2,2,2,64,768]{4,3,0,1,2:T(8,128)(2,1)}, bf16[2,2,2,64,768]{4,3,0,1,2:T(8,128)(2,1)}, u32[]{:S(2)}, u32[]{:S(2)}) %collective-permute-start.7) | collective-permute-done | bytes 786464 | tf_op jit(solution)/shard_map/ppermute | solution.py:339
  618.2 5.1 collective-permute-done.9
  625.5 4.5 fusion.23
  630.6 4.0 collective-permute-done.10
  635.0 8.4 %collective-permute-done.11 = bf16[2,136,768]{2,1,0:T(8,128)(2,1)S(1)} collective-permute-done((bf16[2,136,768]{2,1,0:T(8,128)(2,1)S(1)}, bf16[2,136,768]{2,1,0:T(8,128)(2,1)S(1)}, u32[]{:S(2)}, u32[]{:S(2)}) %collective-permute-start.11) | collective-permute-done | bytes 417824 | tf_op jit(solution)/shard_map/ppermute | solution.py:339
  646.3 5.3 widen_frames.1
  651.6 1.8 collective-permute-done.12
  (516 shorter events, 147.0 us)
Async XLA Ops:
  7.2 206.1 %copy-start = (bf16[1536,1,768]{2,0,1:T(8,128)(2,1)S(1)}, bf16[1536,1,768]{2,0,1:T(8,128)(2,1)}, u32[]{:S(2)}) copy-start(bf16[1536,1,768]{2,0,1:T(8,128)(2,1)} %param.30) | copy-start | bytes 7077892
  7.2 87.7 %copy-start.15 = (bf16[256,1,768]{2,0,1:T(8,128)(2,1)S(1)}, bf16[256,1,768]{2,0,1:T(8,128)(2,1)}, u32[]{:S(2)}) copy-start(bf16[256,1,768]{2,0,1:T(8,128)(2,1)} %param.29) | copy-start | bytes 1179652
  7.2 87.6 %all-gather.8.cloned.1.call-start = ((), (), s32[]{:S(2)}) async-start(), calls=%async_computation.7 | async-start | bytes 6893568 | tf_op jit(solution)/shard_map/all_gather | solution.py:507
  7.3 96.8 %copy-start.97 = (pred[16]{0:T(512)(128)(4,1)}, pred[16]{0:T(512)(128)(4,1)S(1)}, u32[]{:S(2)}) copy-start(pred[16]{0:T(512)(128)(4,1)S(1)} %get-tuple-element.279) | copy-start | bytes 52
  7.3 96.8 %copy-start.99 = (pred[16]{0:T(512)(128)(4,1)}, pred[16]{0:T(512)(128)(4,1)S(1)}, u32[]{:S(2)}) copy-start(pred[16]{0:T(512)(128)(4,1)S(1)} %get-tuple-element.280) | copy-start | bytes 52
  7.3 96.7 %copy-start.101 = (pred[16]{0:T(512)(128)(4,1)}, pred[16]{0:T(512)(128)(4,1)S(1)}, u32[]{:S(2)}) copy-start(pred[16]{0:T(512)(128)(4,1)S(1)} %get-tuple-element.277) | copy-start | bytes 52
  7.3 96.7 %copy-start.103 = (pred[16]{0:T(512)(128)(4,1)}, pred[16]{0:T(512)(128)(4,1)S(1)}, u32[]{:S(2)}) copy-start(pred[16]{0:T(512)(128)(4,1)S(1)} %get-tuple-element.278) | copy-start | bytes 52
  7.4 96.7 %copy-start.105 = (pred[16]{0:T(512)(128)(4,1)}, pred[16]{0:T(512)(128)(4,1)S(1)}, u32[]{:S(2)}) copy-start(pred[16]{0:T(512)(128)(4,1)S(1)} %get-tuple-element.275) | copy-start | bytes 52
  7.4 96.7 %copy-start.107 = (pred[16]{0:T(512)(128)(4,1)}, pred[16]{0:T(512)(128)(4,1)S(1)}, u32[]{:S(2)}) copy-start(pred[16]{0:T(512)(128)(4,1)S(1)} %get-tuple-element.276) | copy-start | bytes 52
  7.4 96.7 %copy-start.109 = (pred[16]{0:T(512)(128)(4,1)}, pred[16]{0:T(512)(128)(4,1)S(1)}, u32[]{:S(2)}) copy-start(pred[16]{0:T(512)(128)(4,1)S(1)} %get-tuple-element.273) | copy-start | bytes 52
  7.4 96.7 %copy-start.111 = (pred[16]{0:T(512)(128)(4,1)}, pred[16]{0:T(512)(128)(4,1)S(1)}, u32[]{:S(2)}) copy-start(pred[16]{0:T(512)(128)(4,1)S(1)} %get-tuple-element.274) | copy-start | bytes 52
  7.4 96.7 %copy-start.113 = (pred[16]{0:T(512)(128)(4,1)}, pred[16]{0:T(512)(128)(4,1)S(1)}, u32[]{:S(2)}) copy-start(pred[16]{0:T(512)(128)(4,1)S(1)} %get-tuple-element.271) | copy-start | bytes 52
  7.4 96.7 %copy-start.115 = (pred[16]{0:T(512)(128)(4,1)}, pred[16]{0:T(512)(128)(4,1)S(1)}, u32[]{:S(2)}) copy-start(pred[16]{0:T(512)(128)(4,1)S(1)} %get-tuple-element.272) | copy-start | bytes 52
  7.5 96.7 %copy-start.117 = (pred[16]{0:T(512)(128)(4,1)}, pred[16]{0:T(512)(128)(4,1)S(1)}, u32[]{:S(2)}) copy-start(pred[16]{0:T(512)(128)(4,1)S(1)} %get-tuple-element.269) | copy-start | bytes 52
  7.5 96.7 %copy-start.119 = (pred[16]{0:T(512)(128)(4,1)}, pred[16]{0:T(512)(128)(4,1)S(1)}, u32[]{:S(2)}) copy-start(pred[16]{0:T(512)(128)(4,1)S(1)} %get-tuple-element.270) | copy-start | bytes 52
  7.5 96.7 %copy-start.121 = (pred[16]{0:T(512)(128)(4,1)}, pred[16]{0:T(512)(128)(4,1)S(1)}, u32[]{:S(2)}) copy-start(pred[16]{0:T(512)(128)(4,1)S(1)} %get-tuple-element.267) | copy-start | bytes 52
  7.5 96.7 %copy-start.123 = (pred[16]{0:T(512)(128)(4,1)}, pred[16]{0:T(512)(128)(4,1)S(1)}, u32[]{:S(2)}) copy-start(pred[16]{0:T(512)(128)(4,1)S(1)} %get-tuple-element.268) | copy-start | bytes 52
  21.5 207.1 %all-gather.10.cloned.1.call-start = ((), (), s32[]{:S(2)}) async-start(), calls=%async_computation.8 | async-start | bytes 13381632 | tf_op jit(solution)/shard_map/all_gather | solution.py:530
  25.7 69.2 %copy-start.52 = (bf16[264,768]{1,0:T(8,128)(2,1)}, bf16[264,768]{1,0:T(8,128)(2,1)S(1)}, u32[]{:S(2)}) copy-start(bf16[264,768]{1,0:T(8,128)(2,1)S(1)} %constant_dynamic-update-slice_fusion.6) | copy-start | bytes 1216516
  95.0 14.6 %copy-start.79 = (f32[256]{0:T(256)}, f32[256]{0:T(256)S(1)}, u32[]{:S(2)}) copy-start(f32[256]{0:T(256)S(1)} %broadcast_multiply_fusion.8) | copy-start | bytes 3076
  95.3 14.4 %copy-start.89 = (f32[256]{0:T(256)}, f32[256]{0:T(256)S(1)}, u32[]{:S(2)}) copy-start(f32[256]{0:T(256)S(1)} %add_rsqrt_fusion.2) | copy-start | bytes 3076
  98.9 10.8 %copy-start.93 = (f32[768]{0:T(1024)}, f32[768]{0:T(1024)S(1)}, u32[]{:S(2)}) copy-start(f32[768]{0:T(1024)S(1)} %reshape.774) | copy-start | bytes 9220
  99.0 10.7 %copy-start.69 = (f32[768]{0:T(1024)}, f32[768]{0:T(1024)S(1)}, u32[]{:S(2)}) copy-start(f32[768]{0:T(1024)S(1)} %reshape.773) | copy-start | bytes 9220
  116.7 59.6 %all-to-all-start = ((bf16[8,3,256,128]{2,3,1,0:T(8,128)(2,1)}), bf16[8,3,256,128]{2,3,1,0:T(8,128)(2,1)}, u32[]{:S(2)}, u32[]{:S(2)}) async-start(bf16[8,3,256,128]{2,3,1,0:T(8,128)(2,1)} %copy.240), calls=%async_computation | async-start | bytes 3145728 | tf_op jit(solution)/shard_map/all_to_all | solution.py:573
  123.4 57.4 %copy-start.68 = (s32[2048]{0:T(1024)}, s32[2048]{0:T(1024)S(1)}, u32[]{:S(2)}) copy-start(s32[2048]{0:T(1024)S(1)} %fusion.66) | copy-start | bytes 24580
  209.4 18.4 %all-to-all-start.1 = ((bf16[8,256,128]{1,2,0:T(8,128)(2,1)}), bf16[8,256,128]{1,2,0:T(8,128)(2,1)S(1)}, u32[]{:S(2)}, u32[]{:S(2)}) async-start(bf16[8,256,128]{1,2,0:T(8,128)(2,1)} %copy.245), calls=%async_computation.1 | async-start | bytes 1048576 | tf_op jit(solution)/shard_map/all_to_all | solution.py:585
  213.0 433.3 %all-gather.6.cloned.1.call-start = ((), (), s32[]{:S(2)}) async-start(), calls=%async_computation.5 | async-start | bytes 2654208 | tf_op jit(solution)/shard_map/all_gather | solution.py:788
  232.2 12.6 %copy-start.7 = (bf16[32,24,768]{2,1,0:T(8,128)(2,1)}, bf16[32,24,768]{2,1,0:T(8,128)(2,1)S(1)}, u32[]{:S(2)}) copy-start(bf16[32,24,768]{2,1,0:T(8,128)(2,1)S(1)} %get-tuple-element.208) | copy-start | bytes 3538948
  245.7 13.4 %copy-start.83 = (f32[256]{0:T(256)}, f32[256]{0:T(256)S(1)}, u32[]{:S(2)}) copy-start(f32[256]{0:T(256)S(1)} %add_rsqrt_fusion.1) | copy-start | bytes 3076
  247.5 11.7 %copy-start.76 = (f32[768]{0:T(1024)S(1)}, f32[768]{0:T(1024)}, u32[]{:S(2)}) copy-start(f32[768]{0:T(1024)} %reshape.782) | copy-start | bytes 9220
  261.1 16.4 %copy-start.1 = (f32[256,768]{1,0:T(8,128)}, f32[256,768]{1,0:T(8,128)S(1)}, u32[]{:S(2)}) copy-start(f32[256,768]{1,0:T(8,128)S(1)} %get-tuple-element.260) | copy-start | bytes 2359300
  261.1 14.2 %slice-start = ((s8[4718592]{0:T(1024)(128)(4,1)}), s8[4194304]{0:T(1024)(128)(4,1)S(1)}, s32[]{:S(2)}) async-start(s8[4718592]{0:T(1024)(128)(4,1)} %bitcast.382), calls=%async_computation.9 | async-start | bytes 8388608
  261.4 11.1 %slice-start.2 = ((s8[4718592]{0:T(1024)(128)(4,1)}), s8[4194304]{0:T(1024)(128)(4,1)S(1)}, s32[]{:S(2)}) async-start(s8[4718592]{0:T(1024)(128)(4,1)} %bitcast.394), calls=%async_computation.11 | async-start | bytes 8388608
  261.6 10.9 %slice-start.3 = ((s8[4718592]{0:T(1024)(128)(4,1)}), s8[524288]{0:T(1024)(128)(4,1)S(1)}, s32[]{:S(2)}) async-start(s8[4718592]{0:T(1024)(128)(4,1)} %bitcast.394), calls=%async_computation.12 | async-start | bytes 1048576
  261.6 10.9 %copy-start.50 = (bf16[256,1,768]{2,1,0:T(2,128)(2,1)S(1)}, bf16[256,1,768]{2,1,0:T(2,128)(2,1)}, u32[]{:S(2)}) copy-start(bf16[256,1,768]{2,1,0:T(2,128)(2,1)} %convert_element_type.585) | copy-start | bytes 1179652
  261.7 13.7 %slice-start.1 = ((s8[4718592]{0:T(1024)(128)(4,1)}), s8[524288]{0:T(1024)(128)(4,1)S(1)}, s32[]{:S(2)}) async-start(s8[4718592]{0:T(1024)(128)(4,1)} %bitcast.382), calls=%async_computation.10 | async-start | bytes 1048576
  308.3 26.9 %collective-permute-start.3 = (bf16[2,2,192,768]{3,2,1,0:T(8,128)(2,1)}, bf16[2,2,192,768]{3,2,1,0:T(8,128)(2,1)}, u32[]{:S(2)}, u32[]{:S(2)}) collective-permute-start(bf16[2,2,192,768]{3,2,1,0:T(8,128)(2,1)} %dynamic-slice_bitcast_fusion.1), channel_id=1, source_target_pairs={{0,2},{1,3},{2,0},{3,1},{4,6},{5,7},{6,4},{7,5},{8,10},{9,11},{10,... | collective-permute-start | bytes 3538952 | tf_op jit(solution)/shard_map/ppermute | solution.py:339
  311.4 27.6 %collective-permute-start = (bf16[2,2,192,768]{3,2,1,0:T(8,128)(2,1)}, bf16[2,2,192,768]{3,2,1,0:T(8,128)(2,1)}, u32[]{:S(2)}, u32[]{:S(2)}) collective-permute-start(bf16[2,2,192,768]{3,2,1,0:T(8,128)(2,1)} %dynamic-slice_bitcast_fusion.2), channel_id=1, source_target_pairs={{0,1},{1,0},{2,3},{3,2},{4,5},{5,4},{6,7},{7,6},{8,9},{9,8},{10,11... | collective-permute-start | bytes 3538952 | tf_op jit(solution)/shard_map/ppermute | solution.py:339
  312.1 26.9 %copy-start.9 = (bf16[1,1536,768]{2,1,0:T(8,128)(2,1)S(1)}, bf16[1,1536,768]{2,1,0:T(8,128)(2,1)}, u32[]{:S(2)}) copy-start(bf16[1,1536,768]{2,1,0:T(8,128)(2,1)} %get-tuple-element.227) | copy-start | bytes 7077892
  337.1 13.7 %collective-permute-start.4 = (bf16[2,192,768]{2,1,0:T(8,128)(2,1)S(1)}, bf16[2,192,768]{2,1,0:T(8,128)(2,1)S(1)}, u32[]{:S(2)}, u32[]{:S(2)}) collective-permute-start(bf16[2,192,768]{2,1,0:T(8,128)(2,1)S(1)} %dynamic-slice_bitcast_fusion.5), channel_id=1, source_target_pairs={{0,1},{1,0},{2,3},{3,2},{4,5},{5,4},{6,7},{7,6},{8,9},{9,8},{10,11... | collective-permute-start | bytes 1769480 | tf_op jit(solution)/shard_map/ppermute | solution.py:339
  340.7 15.4 %collective-permute-start.1 = (bf16[2,192,768]{2,1,0:T(8,128)(2,1)S(1)}, bf16[2,192,768]{2,1,0:T(8,128)(2,1)S(1)}, u32[]{:S(2)}, u32[]{:S(2)}) collective-permute-start(bf16[2,192,768]{2,1,0:T(8,128)(2,1)S(1)} %dynamic-slice_bitcast_fusion.6), channel_id=1, source_target_pairs={{0,2},{1,3},{2,0},{3,1},{4,6},{5,7},{6,4},{7,5},{8,10},{9,11},{10,... | collective-permute-start | bytes 1769480 | tf_op jit(solution)/shard_map/ppermute | solution.py:339
  350.9 23.4 %copy-start.24 = (bf16[32,24,768]{2,1,0:T(8,128)(2,1)S(1)}, bf16[32,24,768]{2,1,0:T(8,128)(2,1)}, u32[]{:S(2)}) copy-start(bf16[32,24,768]{2,1,0:T(8,128)(2,1)} %get-tuple-element.222) | copy-start | bytes 3538948
  351.0 27.9 %copy-start.22 = (bf16[32,24,768]{2,1,0:T(8,128)(2,1)S(1)}, bf16[32,24,768]{2,1,0:T(8,128)(2,1)}, u32[]{:S(2)}) copy-start(bf16[32,24,768]{2,1,0:T(8,128)(2,1)} %get-tuple-element.226) | copy-start | bytes 3538948
  351.0 22.7 %collective-permute-start.5 = (bf16[192,768]{1,0:T(8,128)(2,1)S(1)}, bf16[192,768]{1,0:T(8,128)(2,1)S(1)}, u32[]{:S(2)}, u32[]{:S(2)}) collective-permute-start(bf16[192,768]{1,0:T(8,128)(2,1)S(1)} %dynamic-slice_bitcast_fusion.9), channel_id=1, source_target_pairs={{0,4},{1,5},{2,6},{3,7},{4,0},{5,1},{6,2},{7,3},{8,12},{9,13},{10,... | collective-permute-start | bytes 884744 | tf_op jit(solution)/shard_map/ppermute | solution.py:339
  356.3 21.9 %copy-start.28 = (bf16[2,192,768]{2,1,0:T(8,128)(2,1)}, bf16[2,192,768]{2,1,0:T(8,128)(2,1)S(1)}, u32[]{:S(2)}) copy-start(bf16[2,192,768]{2,1,0:T(8,128)(2,1)S(1)} %fusion.25) | copy-start | bytes 1769476
  356.3 21.8 %collective-permute-start.2 = (bf16[192,768]{1,0:T(8,128)(2,1)S(1)}, bf16[192,768]{1,0:T(8,128)(2,1)S(1)}, u32[]{:S(2)}, u32[]{:S(2)}) collective-permute-start(bf16[192,768]{1,0:T(8,128)(2,1)S(1)} %dynamic-slice_bitcast_fusion.10), channel_id=1, source_target_pairs={{0,4},{1,5},{2,6},{3,7},{4,0},{5,1},{6,2},{7,3},{8,12},{9,13},{10,... | collective-permute-start | bytes 884744 | tf_op jit(solution)/shard_map/ppermute | solution.py:339
  380.2 276.1 %reduce-scatter.2.cloned.1.call-start = ((), (), s32[]{:S(2)}) async-start(), calls=%async_computation.6 | async-start | bytes 13381632 | tf_op jit(solution)/shard_map/reduce_scatter | solution.py:705
  475.8 8.9 %copy-start.85 = (bf16[768]{0:T(1024)(128)(2,1)S(1)}, bf16[768]{0:T(1024)(128)(2,1)}, u32[]{:S(2)}) copy-start(bf16[768]{0:T(1024)(128)(2,1)} %get-tuple-element.238) | copy-start | bytes 4612
  475.8 9.6 %copy-start.127 = (bf16[768]{0:T(1024)(128)(2,1)S(1)}, bf16[768]{0:T(1024)(128)(2,1)}, u32[]{:S(2)}) copy-start(bf16[768]{0:T(1024)(128)(2,1)} %get-tuple-element.194) | copy-start | bytes 4612
  475.8 10.2 %copy-start.125 = (bf16[768]{0:T(1024)(128)(2,1)S(1)}, bf16[768]{0:T(1024)(128)(2,1)}, u32[]{:S(2)}) copy-start(bf16[768]{0:T(1024)(128)(2,1)} %get-tuple-element.193) | copy-start | bytes 4612
  475.9 22.2 %copy-start.34 = (bf16[192,768]{1,0:T(8,128)(2,1)S(1)}, bf16[192,768]{1,0:T(8,128)(2,1)}, u32[]{:S(2)}) copy-start(bf16[192,768]{1,0:T(8,128)(2,1)} %copy-done.33) | copy-start | bytes 884740
  475.9 64.8 %all-to-all-start.3 = ((bf16[8,3,256,128]{2,3,1,0:T(8,128)(2,1)}), bf16[8,3,256,128]{2,3,1,0:T(8,128)(2,1)}, u32[]{:S(2)}, u32[]{:S(2)}) async-start(bf16[8,3,256,128]{2,3,1,0:T(8,128)(2,1)} %pad_maximum_fusion.1), calls=%async_computation.3 | async-start | bytes 3145728 | tf_op jit(solution)/shard_map/all_to_all | solution.py:726
  581.7 6.3 collective-permute-start.6
  593.8 22.7 %collective-permute-start.7 = (bf16[2,2,2,64,768]{4,3,0,1,2:T(8,128)(2,1)}, bf16[2,2,2,64,768]{4,3,0,1,2:T(8,128)(2,1)}, u32[]{:S(2)}, u32[]{:S(2)}) collective-permute-start(bf16[2,2,2,64,768]{4,3,0,1,2:T(8,128)(2,1)} %dynamic-slice_bitcast_fusion.4), channel_id=1, source_target_pairs={{0,16},{8,24},{16,0},{24,8},{1,17},{9,25},{17,1},{25,9},{2,18},{10... | collective-permute-start | bytes 2359304 | tf_op jit(solution)/shard_map/ppermute | solution.py:339
  597.6 25.7 %collective-permute-start.9 = (bf16[2,2,2,72,768]{4,3,1,2,0:T(8,128)(2,1)}, bf16[2,2,2,72,768]{4,3,1,2,0:T(8,128)(2,1)}, u32[]{:S(2)}, u32[]{:S(2)}) collective-permute-start(bf16[2,2,2,72,768]{4,3,1,2,0:T(8,128)(2,1)} %dynamic-slice_bitcast_fusion.3), channel_id=1, source_target_pairs={{0,1},{1,0},{2,3},{3,2},{4,5},{5,4},{6,7},{7,6},{8,9},{9,8},{10,11... | collective-permute-start | bytes 2654216 | tf_op jit(solution)/shard_map/ppermute | solution.py:339
  599.0 24.3 %copy-start.13 = (bf16[2,2,2,2,72,768]{5,4,1,2,0,3:T(8,128)(2,1)S(1)}, bf16[2,2,2,2,72,768]{5,4,1,2,0,3:T(8,128)(2,1)}, u32[]{:S(2)}) copy-start(bf16[2,2,2,2,72,768]{5,4,1,2,0,3:T(8,128)(2,1)} %copy-done.12) | copy-start | bytes 5308420
  618.1 12.3 %collective-permute-start.8 = (bf16[2,2,64,768]{3,2,0,1:T(8,128)(2,1)S(1)}, bf16[2,2,64,768]{3,2,0,1:T(8,128)(2,1)S(1)}, u32[]{:S(2)}, u32[]{:S(2)}) collective-permute-start(bf16[2,2,64,768]{3,2,0,1:T(8,128)(2,1)S(1)} %dynamic-slice_bitcast_fusion.8), channel_id=1, source_target_pairs={{0,1},{1,0},{2,3},{3,2},{4,5},{5,4},{6,7},{7,6},{8,9},{9,8},{10,11... | collective-permute-start | bytes 1179656 | tf_op jit(solution)/shard_map/ppermute | solution.py:339
  624.8 9.9 %collective-permute-start.10 = (bf16[2,2,72,768]{3,2,0,1:T(8,128)(2,1)S(1)}, bf16[2,2,72,768]{3,2,0,1:T(8,128)(2,1)S(1)}, u32[]{:S(2)}, u32[]{:S(2)}) collective-permute-start(bf16[2,2,72,768]{3,2,0,1:T(8,128)(2,1)S(1)} %dynamic-slice_bitcast_fusion.7), channel_id=1, source_target_pairs={{0,16},{8,24},{16,0},{24,8},{1,17},{9,25},{17,1},{25,9},{2,18},{10... | collective-permute-start | bytes 1327112 | tf_op jit(solution)/shard_map/ppermute | solution.py:339
  630.6 13.7 %copy-start.51 = (f32[256,768]{1,0:T(8,128)S(1)}, f32[256,768]{1,0:T(8,128)}, u32[]{:S(2)}) copy-start(f32[256,768]{1,0:T(8,128)} %get-tuple-element.264) | copy-start | bytes 2359300
  630.6 13.7 %copy-start.72 = (f32[768]{0:T(1024)S(1)}, f32[768]{0:T(1024)}, u32[]{:S(2)}) copy-start(f32[768]{0:T(1024)} %copy-done.69) | copy-start | bytes 9220
  630.6 13.7 %copy-start.82 = (f32[256]{0:T(256)S(1)}, f32[256]{0:T(256)}, u32[]{:S(2)}) copy-start(f32[256]{0:T(256)} %copy-done.79) | copy-start | bytes 3076
  630.6 13.7 %copy-start.92 = (f32[256]{0:T(256)S(1)}, f32[256]{0:T(256)}, u32[]{:S(2)}) copy-start(f32[256]{0:T(256)} %copy-done.89) | copy-start | bytes 3076
  634.8 8.5 %collective-permute-start.11 = (bf16[2,136,768]{2,1,0:T(8,128)(2,1)S(1)}, bf16[2,136,768]{2,1,0:T(8,128)(2,1)S(1)}, u32[]{:S(2)}, u32[]{:S(2)}) collective-permute-start(bf16[2,136,768]{2,1,0:T(8,128)(2,1)S(1)} %fusion.49), channel_id=1, source_target_pairs={{0,2},{1,3},{2,0},{3,1},{4,6},{5,7},{6,4},{7,5},{8,10},{9,11},{10,... | collective-permute-start | bytes 1253384 | tf_op jit(solution)/shard_map/ppermute | solution.py:339
  644.2 9.3 %collective-permute-start.12 = (bf16[136,768]{1,0:T(8,128)(2,1)}, bf16[136,768]{1,0:T(8,128)(2,1)}, u32[]{:S(2)}, u32[]{:S(2)}) collective-permute-start(bf16[136,768]{1,0:T(8,128)(2,1)} %dynamic-slice_bitcast_fusion.11), channel_id=1, source_target_pairs={{0,4},{1,5},{2,6},{3,7},{4,0},{5,1},{6,2},{7,3},{8,12},{9,13},{10,... | collective-permute-start | bytes 626696 | tf_op jit(solution)/shard_map/ppermute | solution.py:339
  (92 other events, 229.6 us)
Sparse Core Ops, SparseCore 0:
  21.6 73.2 all-gather.7
  97.8 117.7 all-gather.9
  380.3 62.1 all-gather.5
  448.3 171.6 reduce-scatter.1
where the time goes:
time: 677 us; the launch traced here: 667 us
  waiting for transfers between devices  249 us (37%)
  local copies, waits for them, and re-layouts  152 us (22%)
  Pallas kernels  87.1 us (13%)
  matrix products  63.9 us (9%)
  other arithmetic  38.3 us (6%)
  blocking collectives  34.8 us (5%)
  starting transfers between devices  24.5 us (4%)
  between operations  16.8 us (2%)
    ppermute x13, waiting for transfers between devices, halve(): received = lax.ppermute(sent, axis_name, pairs)  94.1 us
    all_gather x1, waiting for transfers between devices, local_heads(): first = lax.all_gather(first_packed, ('dp', 'seq'), axis=0, tiled=False)  69.2 us
    all_to_all x1, waiting for transfers between devices, local_heads(): lax.all_to_all(jnp.stack(tuple((to_pairs(rows, seq_count) for rows in (qu...  40.6 us
    all_to_all x1, waiting for transfers between devices, local_heads(): grad_triple = lax.all_to_all(grad_blocks, 'seq', 0, 0)  38.4 us
    all_to_all x1, blocking collectives, local_heads(): head_grad = lax.all_to_all(head_blocks, 'seq', 0, 0)  34.8 us
    unnamed x295, local copies, waits for them, and re-layouts  34 us
    dot_general x10, matrix products, project(): return jnp.dot(left_rows, matrix, preferred_element_type=jnp.float32)  33.3 us
    pallas_call x1, Pallas kernels, self_backward(): pl.pallas_call(self_backward_body, grid=(length // QUERY_BLOCK,), in_spec...  26.1 us
  transfers between devices with their start and end apart: 20, of which 16 were waited for; matrix products, arithmetic and copies ran while one was open for 27% of the time, Pallas kernels for 8%

commit v1 on v0

--- a/solution.py
+++ b/solution.py
@@ -42,6 +42,10 @@
     return jnp.sum(grad_rows.astype(jnp.float32), axis=0)
 
 
+def row_sums(grad_rows):
+    return jnp.sum(grad_rows.astype(jnp.float32), axis=0, keepdims=True)
+
+
 def exact_gelu(inputs):
     return jax.nn.gelu(inputs, approximate=False)
 
@@ -128,22 +132,37 @@
     return (key_pos <= query_pos) | same_piece
 
 
+def key_rows_at(ref, key_block):
+    parts = KEY_BLOCK // QUERY_BLOCK
+    return ref[pl.ds(key_block * parts, parts), 0].reshape(KEY_BLOCK, PAIR)
+
+
+def exchange_specs(owners):
+    return [
+        pl.BlockSpec((1, 1, QUERY_BLOCK, PAIR), lambda index: (index, 0, 0, 0)),
+        pl.BlockSpec((owners, 1, QUERY_BLOCK, PAIR), lambda index: (0, 1, 0, 0)),
+        pl.BlockSpec((owners, 1, QUERY_BLOCK, PAIR), lambda index: (0, 2, 0, 0)),
+    ]
+
+
 def key_block_range(block, key_rows):
     full = block * QUERY_BLOCK // KEY_BLOCK
     last = ((block + 2) * QUERY_BLOCK + KEY_BLOCK - 1) // KEY_BLOCK
     return (full, jnp.minimum(last, key_rows // KEY_BLOCK))
 
 
-def self_forward_body(query_ref, key_ref, value_ref, column_ref, row_ref, out_ref, log_ref):
+def self_forward_body(
+    query_ref, key_ref, value_ref, column_ref, row_ref, out_ref, log_ref, low_ref
+):
     block = pl.program_id(0)
-    queries = stack_pair(query_ref[...] * jnp.bfloat16(0.125))
+    queries = stack_pair(query_ref[0, 0] * jnp.bfloat16(0.125))
     query_label = column_ref[...]
 
     def step(key_block, state, masked):
         start = pl.multiple_of(key_block * KEY_BLOCK, KEY_BLOCK)
         here = pl.ds(start, KEY_BLOCK)
         row_max, row_total, weighted = state
-        scores = dot_rows(queries, key_ref[here, :])
+        scores = dot_rows(queries, key_rows_at(key_ref, key_block))
         if masked:
             shape = (QUERY_BLOCK, KEY_BLOCK)
             allowed = block_allowed(
@@ -163,7 +182,9 @@
         exp_terms = jnp.exp(scores - new_max)
         factor = jnp.exp(row_max - new_max)
         row_total = row_total * factor + jnp.sum(exp_terms, axis=1, keepdims=True)
-        weighted = weighted * factor + dot_plain(rounded(exp_terms), value_ref[here, :])
+        weighted = weighted * factor + dot_plain(
+            rounded(exp_terms), key_rows_at(value_ref, key_block)
+        )
         return (new_max, row_total, weighted)
 
     state = (
@@ -171,33 +192,41 @@
         jnp.zeros((2 * QUERY_BLOCK, 1), jnp.float32),
         jnp.zeros((2 * QUERY_BLOCK, PAIR), jnp.float32),
     )
-    full, last = key_block_range(block, key_ref.shape[0])
+    full, last = key_block_range(block, key_ref.shape[0] * QUERY_BLOCK)
     state = lax.fori_loop(0, full, lambda index, state: step(index, state, False), state)
     state = lax.fori_loop(full, last, lambda index, state: step(index, state, True), state)
     row_max, row_total, weighted = state
-    out_ref[...] = join_stack(weighted / row_total)
+    attended = join_stack(weighted / row_total)
+    out_ref[...] = attended
+    low_ref[0] = rounded(attended)
     log_ref[...] = join_stack(jnp.broadcast_to(row_max + jnp.log(row_total), weighted.shape))
 
 
-def self_forward(queries, keys, values, labels):
-    length = queries.shape[0]
+def self_forward(triple, labels):
+    owners = triple.shape[0]
+    length = owners * QUERY_BLOCK
     block_spec = pl.BlockSpec((QUERY_BLOCK, PAIR), lambda index: (index, 0))
-    whole_spec = pl.BlockSpec((length, PAIR), lambda index: (0, 0))
     result = jax.ShapeDtypeStruct((length, PAIR), jnp.float32)
     return pl.pallas_call(
         self_forward_body,
-        grid=(length // QUERY_BLOCK,),
-        in_specs=[
-            block_spec,
-            whole_spec,
-            whole_spec,
+        grid=(owners,),
+        in_specs=exchange_specs(owners)
+        + [
             pl.BlockSpec((QUERY_BLOCK, 1), lambda index: (index, 0)),
             pl.BlockSpec((1, length), lambda index: (0, 0)),
         ],
-        out_specs=[block_spec, block_spec],
-        out_shape=[result, result],
+        out_specs=[
+            block_spec,
+            block_spec,
+            pl.BlockSpec((1, QUERY_BLOCK, PAIR), lambda index: (index, 0, 0)),
+        ],
+        out_shape=[
+            result,
+            result,
+            jax.ShapeDtypeStruct((owners, QUERY_BLOCK, PAIR), jnp.bfloat16),
+        ],
         name="self_forward",
-    )(queries, keys, values, labels[:, None], labels[None, :])
+    )(triple, triple, triple, labels[:, None], labels[None, :])
 
 
 def self_backward_body(
@@ -209,9 +238,7 @@
     out_ref,
     log_ref,
     grad_ref,
-    grad_query_ref,
-    grad_key_ref,
-    grad_value_ref,
+    triple_ref,
     key_sum,
     value_sum,
 ):
@@ -223,9 +250,9 @@
         key_sum[...] = jnp.zeros_like(key_sum)
         value_sum[...] = jnp.zeros_like(value_sum)
 
-    queries = stack_pair(query_ref[...] * jnp.bfloat16(0.125))
+    queries = stack_pair(query_ref[0, 0] * jnp.bfloat16(0.125))
     query_label = row_ref[...]
-    grad_rows = grad_ref[...]
+    grad_rows = grad_ref[0]
     grads = stack_pair(grad_rows)
     products = stack_pair(grad_rows.astype(jnp.float32) * out_ref[...])
     delta = jnp.sum(jnp.transpose(products), axis=0, keepdims=True)
@@ -235,7 +262,7 @@
     def step(key_block, query_sum, masked):
         start = pl.multiple_of(key_block * KEY_BLOCK, KEY_BLOCK)
         here = pl.ds(start, KEY_BLOCK)
-        keys = key_ref[here, :]
+        keys = key_rows_at(key_ref, key_block)
         scores = dot_rows(keys, queries)
         if masked:
             shape = (KEY_BLOCK, QUERY_BLOCK)
@@ -253,50 +280,96 @@
                 axis=1,
             )
         probs = jnp.exp(scores - logs)
-        grad_probs = dot_rows(value_ref[here, :], grads)
+        grad_probs = dot_rows(key_rows_at(value_ref, key_block), grads)
         grad_scores = rounded(probs * (grad_probs - delta))
         key_sum[here, :] = key_sum[here, :] + dot_plain(grad_scores, queries)
         value_sum[here, :] = value_sum[here, :] + dot_plain(rounded(probs), grads)
         return query_sum + dot_columns(grad_scores, keys)
 
     query_sum = jnp.zeros((2 * QUERY_BLOCK, PAIR), jnp.float32)
-    full, last = key_block_range(block, key_ref.shape[0])
+    full, last = key_block_range(block, key_ref.shape[0] * QUERY_BLOCK)
     query_sum = lax.fori_loop(0, full, lambda index, total: step(index, total, False), query_sum)
     query_sum = lax.fori_loop(full, last, lambda index, total: step(index, total, True), query_sum)
-    grad_query_ref[...] = rounded(join_stack(query_sum) * 0.125)
+    triple_ref[block, 0] = rounded(join_stack(query_sum) * 0.125)
 
     @pl.when(block == block_count - 1)
     def finish():
-        grad_key_ref[...] = rounded(key_sum[...])
-        grad_value_ref[...] = rounded(value_sum[...])
-
-
-def self_backward(queries, keys, values, labels, attended, log_total, grad_attended):
-    length = queries.shape[0]
+        for owner in range(triple_ref.shape[0]):
+            rows = slice(owner * QUERY_BLOCK, (owner + 1) * QUERY_BLOCK)
+            triple_ref[owner, 1] = rounded(key_sum[rows, :])
+            triple_ref[owner, 2] = rounded(value_sum[rows, :])
+
+
+def self_backward(triple, labels, attended, log_total, grad_attended):
+    owners = triple.shape[0]
+    length = owners * QUERY_BLOCK
     block_spec = pl.BlockSpec((QUERY_BLOCK, PAIR), lambda index: (index, 0))
-    whole_spec = pl.BlockSpec((length, PAIR), lambda index: (0, 0))
-    result = jax.ShapeDtypeStruct((length, PAIR), jnp.bfloat16)
     return pl.pallas_call(
         self_backward_body,
-        grid=(length // QUERY_BLOCK,),
-        in_specs=[
-            block_spec,
-            whole_spec,
-            whole_spec,
+        grid=(owners,),
+        in_specs=exchange_specs(owners)
+        + [
             pl.BlockSpec((length, 1), lambda index: (0, 0)),
             pl.BlockSpec((1, QUERY_BLOCK), lambda index: (0, index)),
             block_spec,
             block_spec,
-            block_spec,
+            pl.BlockSpec((1, QUERY_BLOCK, PAIR), lambda index: (index, 0, 0)),
         ],
-        out_specs=[block_spec, whole_spec, whole_spec],
-        out_shape=[result, result, result],
+        out_specs=pl.BlockSpec(triple.shape, lambda index: (0, 0, 0, 0)),
+        out_shape=jax.ShapeDtypeStruct(triple.shape, jnp.bfloat16),
         scratch_shapes=[
             pltpu.VMEM((length, PAIR), jnp.float32),
             pltpu.VMEM((length, PAIR), jnp.float32),
         ],
         name="self_backward",
-    )(queries, keys, values, labels[:, None], labels[None, :], attended, log_total, grad_attended)
+    )(
+        triple,
+        triple,
+        triple,
+        labels[:, None],
+        labels[None, :],
+        attended,
+        log_total,
+        grad_attended,
+    )
+
+
+def pack_body(*refs):
+    row_refs, wide_ref, out_ref, stacked = refs[:-3], refs[-3], refs[-2], refs[-1]
+    stacked[...] = jnp.zeros_like(stacked)
+    for slot, ref in enumerate(row_refs):
+        stacked[slot : slot + 1, :] = ref[...]
+    rows = stacked[...]
+    wide = jnp.broadcast_to(wide_ref[...], (16, wide_ref.shape[1]))
+    owners = out_ref.shape[0]
+    narrow, long = rows.shape[1] // owners, wide.shape[1] // owners
+    lanes = lax.broadcasted_iota(jnp.int32, (16, 128), 1)
+    slots = lax.broadcasted_iota(jnp.int32, (16, 128), 0)
+    out_ref[...] = jnp.zeros_like(out_ref)
+
+    def window(source, start, width):
+        base = min(start // 128 * 128, source.shape[1] - 256)
+        offset = start - base
+        moved = source[:, base : base + 256]
+        if offset:
+            moved = pltpu.roll(moved, 256 - offset, 1)
+        return jnp.where(lanes < width, moved[:, :128], 0.0)
+
+    for owner in range(owners):
+        block = window(rows, owner * narrow, narrow)
+        long_block = window(wide, owner * long, long)
+        block = jnp.where(slots == len(row_refs), long_block, block)
+        out_ref[owner, :, :128] = rounded(block)
+
+
+def pack_vectors(vectors, wide, owners):
+    rows = tuple(vector.reshape(1, -1) for vector in vectors)
+    return pl.pallas_call(
+        pack_body,
+        out_shape=jax.ShapeDtypeStruct((owners, 16, D), jnp.bfloat16),
+        scratch_shapes=[pltpu.VMEM((16, D), jnp.float32)],
+        name="pack_vectors",
+    )(*rows, wide.reshape(1, -1))
 
 
 def widen_body(frame_ref, out_ref):
@@ -578,13 +651,8 @@
         0,
         0,
     )
-    head_queries, head_keys, head_values = (
-        head_triple[:, slot].reshape(full_length, PAIR) for slot in range(3)
-    )
-    head_attended, head_log = self_forward(head_queries, head_keys, head_values, labels)
-    attended_blocks = lax.all_to_all(
-        rounded(head_attended).reshape(seq_count, local_len, PAIR), "seq", 0, 0
-    )
+    head_attended, head_log, head_low = self_forward(head_triple, labels)
+    attended_blocks = lax.all_to_all(head_low, "seq", 0, 0)
     attended_self_low = from_pairs(attended_blocks)
     middle_rows = (
         input_rows
@@ -630,14 +698,14 @@
     grad_result = out_grad.reshape(token_count, D)
     grad_mlp_low = rounded(grad_result)
     grad_fc_out_weight = weight_grad(activated_low, grad_mlp_low)
-    grad_fc_out_bias = column_sums(grad_mlp_low)
+    grad_fc_out_bias = row_sums(grad_mlp_low)
     grad_activated = project_back(grad_mlp_low, back_fc_out)
     grad_hidden_low = rounded(gelu_pull(grad_activated)[0])
     grad_fc_in_blocks = tuple(
         weight_grad(normed_mlp_low, grad_hidden_low[:, part * D : (part + 1) * D])
         for part in range(wide_parts)
     )
-    grad_fc_in_bias = column_sums(grad_hidden_low)
+    grad_fc_in_bias = row_sums(grad_hidden_low)
     grad_normed_mlp = project_back(grad_hidden_low, back_fc_in)
     grad_rows_mlp, grad_mlp_gain, grad_mlp_shift = norm_backward(
         grad_normed_mlp, scaled_mlp, inverse_mlp, full_mlp_gain.astype(jnp.float32)
@@ -651,7 +719,7 @@
     )
     grad_cross_low = rounded(grad_after)
     grad_cross_out_weight = weight_grad(attended_cross_low, grad_cross_low)
-    grad_cross_out_bias = column_sums(grad_cross_low)
+    grad_cross_out_bias = row_sums(grad_cross_low)
     grad_attended_cross = rounded(project_back(grad_cross_low, back_cross_out))
     grad_cross_queries, grad_memory_kv = cross_backward(
         memory_lengths,
@@ -675,9 +743,9 @@
     )
     grad_cross_key_weight = weight_grad(memory_part, part_flat_keys)
     grad_cross_value_weight = weight_grad(memory_part, part_flat_values)
-    grad_cross_value_bias = column_sums(part_flat_values)
+    grad_cross_value_bias = row_sums(part_flat_values)
     grad_cross_query_weight = weight_grad(normed_cross_low, grad_cross_queries)
-    grad_cross_query_bias = column_sums(grad_cross_queries)
+    grad_cross_query_bias = row_sums(grad_cross_queries)
     grad_normed_cross = project_back(grad_cross_queries, back_cross_query)
     grad_rows_cross, grad_cross_gain, grad_cross_shift = norm_backward(
         grad_normed_cross, scaled_cross, inverse_cross, full_cross_gain.astype(jnp.float32)
@@ -691,7 +759,7 @@
     )
     grad_self_low = rounded(grad_middle)
     grad_attn_out_weight = weight_grad(attended_self_low, grad_self_low)
-    grad_attn_out_bias = column_sums(grad_self_low)
+    grad_attn_out_bias = row_sums(grad_self_low)
     early_grads = jnp.concatenate(
         (
             *(owner_rows(block) for block in grad_fc_in_blocks),
@@ -716,22 +784,16 @@
     grad_attended_self = rounded(project_back(grad_self_low, back_self_out))
     head_blocks = to_pairs(grad_attended_self, seq_count)
     head_grad = lax.all_to_all(head_blocks, "seq", 0, 0)
-    head_grad = head_grad.reshape(full_length, PAIR)
-    head_grads = self_backward(
-        head_queries, head_keys, head_values, labels, head_attended, head_log, head_grad
-    )
-    grad_blocks = jnp.stack(
-        tuple(part.reshape(seq_count, local_len, PAIR) for part in head_grads), axis=1
-    )
+    grad_blocks = self_backward(head_triple, labels, head_attended, head_log, head_grad)
     grad_triple = lax.all_to_all(grad_blocks, "seq", 0, 0)
     grad_query_low, grad_key_low, grad_value_low = (
         from_pairs(grad_triple[:, slot]) for slot in range(3)
     )
     grad_query_weight = weight_grad(normed_self_low, grad_query_low)
-    grad_query_bias = column_sums(grad_query_low)
+    grad_query_bias = row_sums(grad_query_low)
     grad_key_weight = weight_grad(normed_self_low, grad_key_low)
     grad_value_weight = weight_grad(normed_self_low, grad_value_low)
-    grad_value_bias = column_sums(grad_value_low)
+    grad_value_bias = row_sums(grad_value_low)
     grad_normed_self = (
         project_back(grad_query_low, back_query)
         + project_back(grad_key_low, back_key)
@@ -741,27 +803,24 @@
         grad_normed_self, scaled_self, inverse_self, full_self_gain.astype(jnp.float32)
     )
     token_grad = (grad_middle + grad_rows_self).reshape(local_len, batch_count, D)
-    late_block = place_rows(
-        tuple(
-            vector.reshape(owners, -1)
-            for vector in (
-                grad_self_gain,
-                grad_self_shift,
-                grad_query_bias,
-                grad_value_bias,
-                grad_attn_out_bias,
-                grad_cross_gain,
-                grad_cross_shift,
-                grad_cross_query_bias,
-                grad_cross_value_bias,
-                grad_cross_out_bias,
-                grad_mlp_gain,
-                grad_mlp_shift,
-                grad_fc_out_bias,
-                grad_fc_in_bias,
-            )
+    late_block = pack_vectors(
+        (
+            grad_self_gain,
+            grad_self_shift,
+            grad_query_bias,
+            grad_value_bias,
+            grad_attn_out_bias,
+            grad_cross_gain,
+            grad_cross_shift,
+            grad_cross_query_bias,
+            grad_cross_value_bias,
+            grad_cross_out_bias,
+            grad_mlp_gain,
+            grad_mlp_shift,
+            grad_fc_out_bias,
         ),
-        16,
+        grad_fc_in_bias,
+        owners,
     )
     late_grads = jnp.concatenate(
         (

time: 677 us -> 658 us (0.972)
  local copies, waits for them, and re-layouts: 152 us -> 118 us
  waiting for transfers between devices: 249 us -> 265 us
  other arithmetic: 38.3 us -> 31.2 us
    ppermute x13, waiting for transfers between devices: 94.1 us -> 112 us  [halve(): received = lax.ppermute(sent, axis_name, pairs)]
    broadcast_in_dim x28 -> x5, local copies, waits for them, and re-layouts: 17.8 us -> 2.96 us  [row_sums(): return jnp.sum(grad_rows.astype(jnp.float32), axis=0, keepdims=True)]
    all_to_all x1, waiting for transfers between devices: 38.4 us -> 25.4 us  [local_heads(): grad_triple = lax.all_to_all(grad_blocks, 'seq', 0, 0)]
    all_to_all x1, waiting for transfers between devices: 40.6 us -> 52.1 us  [local_heads(): lax.all_to_all(jnp.stack(tuple((to_pairs(rows, seq_count) for rows in (qu...]
    slice x6 -> x0, local copies, waits for them, and re-layouts: 9.78 us -> none  [the longest x4 7.54 us: local_heads(): head_triple[:, slot].reshape(full_length, PAIR)]
    transpose x0 -> x6, local copies, waits for them, and re-layouts: none -> 9.75 us  [from_pairs(): return jnp.transpose(kept, (1, 0, 2)).reshape(kept.shape[1], D)]
    convert_element_type x14 -> x0, local copies, waits for them, and re-layouts: 8.77 us -> none  [place_rows(): wide = jnp.pad(vector.astype(jnp.bfloat16), padding)[..., None, :]]
    pad x28 -> x14, local copies, waits for them, and re-layouts: 17.4 us -> 9.37 us  [place_rows(): wide = jnp.pad(vector.astype(jnp.bfloat16), padding)[..., None, :]]
  transfers between devices with their start and end apart: 20 -> 20, of which waited for: 16 -> 16; matrix products, arithmetic and copies ran while one was open for 27% -> 22% of each run, Pallas kernels for 8% -> 9%
where the time goes in v1:
time: 658 us; the launch traced here: 649 us
  waiting for transfers between devices  265 us (40%)
  local copies, waits for them, and re-layouts  118 us (18%)
  Pallas kernels  89 us (14%)
  matrix products  64.7 us (10%)
  blocking collectives  35.3 us (5%)
  other arithmetic  31.2 us (5%)
  starting transfers between devices  30 us (5%)
  between operations  16 us (2%)
    ppermute x13, waiting for transfers between devices, halve(): received = lax.ppermute(sent, axis_name, pairs)  112 us
    all_gather x1, waiting for transfers between devices, local_heads(): first = lax.all_gather(first_packed, ('dp', 'seq'), axis=0, tiled=False)  69.2 us
    all_to_all x1, waiting for transfers between devices, local_heads(): lax.all_to_all(jnp.stack(tuple((to_pairs(rows, seq_count) for rows in (qu...  52.1 us
    all_to_all x1, blocking collectives, local_heads(): head_grad = lax.all_to_all(head_blocks, 'seq', 0, 0)  35.3 us
    unnamed x202, local copies, waits for them, and re-layouts  33.4 us
    dot_general x10, matrix products, project(): return jnp.dot(left_rows, matrix, preferred_element_type=jnp.float32)  32.4 us
    pallas_call x1, Pallas kernels, self_backward(): pl.pallas_call(self_backward_body, grid=(owners,), in_specs=exchange_spec...  26.2 us
    all_to_all x1, waiting for transfers between devices, local_heads(): grad_triple = lax.all_to_all(grad_blocks, 'seq', 0, 0)  25.4 us
  transfers between devices with their start and end apart: 20, of which 16 were waited for; matrix products, arithmetic and copies ran while one was open for 22% of the time, Pallas kernels for 9%

profile of v1, /device:TPU:0, one launch (start us, length us, event | category | flops | bytes accessed | tf_op | source)
XLA Modules:
  0.0 648.6 jit_solution(13460573362990349339)
XLA Ops:
  25.6 69.2 %all-gather.8.cloned.1.call-done = bf16[4352,768]{1,0:T(8,128)(2,1)} async-done(((bf16[136,768]{1,0:T(8,128)(2,1)}), bf16[4352,768]{1,0:T(8,128)(2,1)}) %all-gather.8.cloned.1.call-update) | async-done | bytes 6684688 | tf_op jit(solution)/shard_map/all_gather | solution.py:580
  97.3 2.7 fusion.84
  100.9 5.1 fusion.85
  108.0 1.8 fusion.19
  112.0 2.6 convolution_convert_fusion.16
  114.6 1.9 copy.152
  116.5 1.9 copy.153
  120.9 4.4 all-to-all-start
  140.0 52.1 %all-to-all-done.query_ref.key_ref.value_ref = bf16[8,3,256,128]{3,2,1,0:T(8,128)(2,1)} async-done(((bf16[8,3,256,128]{3,2,1,0:T(8,128)(2,1)}), bf16[8,3,256,128]{3,2,1,0:T(8,128)(2,1)}, u32[]{:S(2)}, u32[]{:S(2)}) %all-to-all-start) | async-done | bytes 1572896 | tf_op jit(solution)/shard_map/all_to_all | solution.py:646
  192.2 23.1 %self_forward.1 = (f32[2048,128]{1,0:T(8,128)}, f32[2048,128]{1,0:T(8,128)}, bf16[8,256,128]{2,1,0:T(8,128)(2,1)}) custom-call(bf16[8,3,256,128]{3,2,1,0:T(8,128)(2,1)} %all-to-all-done.query_ref.key_ref.value_ref, bf16[8,3,256,128]{3,2,1,0:T(8,128)(2,1)} %all-to-all-done.query_ref.key_ref.value_ref, ...), custom_call_target="tpu_custom_call" | custom-call | tf_op jit(solution)/shard_map/self_forward/pallas_call | solution.py:210
  215.3 4.8 all-to-all-start.1
  220.3 4.8 fusion.7.key_ref
  225.1 3.4 fusion.8.value_ref
  228.5 6.2 all-to-all-done.1
  235.5 1.9 copy.158
  237.4 3.7 fusion.83
  241.1 7.0 %fusion.82 = (bf16[32,96,768]{2,1,0:T(8,128)(2,1)}, bf16[32,96,768]{2,1,0:T(8,128)(2,1)S(1)}) fusion(bf16[32,264,768]{2,1,0:T(8,128)(2,1)} %bitcast.350), kind=kLoop, calls=%fused_computation.268 | loop fusion | bytes 18874368 | tf_op jit(solution)/shard_map/slice | solution.py:616
  248.0 2.3 copy.170
  250.4 3.2 copy.209
  256.2 11.6 %cross_forward.1 = (bf16[256,768]{1,0:T(8,128)(2,1)}, f32[256,768]{1,0:T(8,128)}) custom-call(s32[1]{0:T(128)S(6)} %copy.269.length_ref, bf16[256,768]{1,0:T(8,128)(2,1)} %fusion.21.query_ref, bf16[1536,768]{1,0:T(8,128)(2,1)} %fusion.7.key_ref, bf16[1536,768]{1,0:T(8,128)(2,1)} %fusion.8.value_ref), custom_call_target="tpu_custom_call" | custom-call | tf_op jit(solution)/shard_map/cross_forward/pallas_call | solution.py:441
  267.9 2.0 fusion.89
  270.4 10.9 %multiply_convert_fusion = (bf16[256,3072]{1,0:T(8,128)(2,1)}, f32[256,3072]{1,0:T(8,128)S(1)}, f32[256,3072]{1,0:T(8,128)S(1)}) fusion(f32[3072]{0:T(1024)S(1)} %copy-done.64, bf16[256,768]{1,0:T(8,128)(2,1)S(1)} %add_convert_fusion.2, bf16[768,3072]{1,0:T(8,128)(2,1)} %bitcast.372), kind=kOutput, calls=%fused_computation.13 | convolution fusion | flops 1259864064 | bytes 12988416 | tf_op jit(solution)/shard_map/dot_general | solution.py:26
  281.3 2.8 convert_reduce_fusion
  284.1 2.1 multiply_reduce_fusion
  289.3 20.9 %cross_backward.1 = (bf16[256,768]{1,0:T(8,128)(2,1)}, bf16[2,1536,768]{2,1,0:T(8,128)(2,1)}) custom-call(s32[1]{0:T(128)S(6)} %copy.269.length_ref, bf16[256,768]{1,0:T(8,128)(2,1)} %fusion.21.query_ref, bf16[1536,768]{1,0:T(8,128)(2,1)} %fusion.7.key_ref, bf16[1536,768]{1,0:T(8,128)(2,1)} %fusion.8.value_ref, f32[256,768]{1,0:T(8,128)} %get-tuple-element.38.log_ref, ...), custom_call_target="tpu_custom_call" | custom-call | tf_op jit(solution)/shard_map/cross_backward/pallas_call | solution.py:484
  310.2 4.1 fusion.86
  317.5 2.4 dynamic-slice_bitcast_fusion.1
  320.7 22.8 %collective-permute-done.3 = bf16[2,2,192,768]{3,2,1,0:T(8,128)(2,1)} collective-permute-done((bf16[2,2,192,768]{3,2,1,0:T(8,128)(2,1)}, bf16[2,2,192,768]{3,2,1,0:T(8,128)(2,1)}, u32[]{:S(2)}, u32[]{:S(2)}) %collective-permute-start.3) | collective-permute-done | bytes 1179680 | tf_op jit(solution)/shard_map/ppermute | solution.py:412
  343.4 1.9 fusion.9
  345.4 2.1 collective-permute-start.4
  350.3 2.5 convolution_convert_fusion.7
  352.8 6.4 collective-permute-done.4
  359.5 2.4 collective-permute-start.5
  361.9 2.6 collective-permute-done.1
  364.8 2.3 collective-permute-start.2
  367.1 15.1 %collective-permute-done.5 = bf16[192,768]{1,0:T(8,128)(2,1)S(1)} collective-permute-done((bf16[192,768]{1,0:T(8,128)(2,1)S(1)}, bf16[192,768]{1,0:T(8,128)(2,1)S(1)}, u32[]{:S(2)}, u32[]{:S(2)}) %collective-permute-start.5) | collective-permute-done | bytes 294944 | tf_op jit(solution)/shard_map/ppermute | solution.py:412
  383.0 3.7 collective-permute-done.2
  399.2 2.4 constant_dynamic-update-slice_fusion.20
  409.0 1.8 convolution_convert_fusion.14
  412.9 35.3 %all_to_all.20.grad_ref = bf16[8,256,128]{2,1,0:T(8,128)(2,1)} all-to-all(bf16[8,256,128]{2,1,0:T(8,128)(2,1)S(1)} %pad.74), channel_id=1, replica_groups=mesh['dp'=4,'seq'=8] {'seq'}, dimensions={0} | all-to-all | bytes 1048576 | tf_op jit(solution)/shard_map/all_to_all | solution.py:786
  448.3 26.2 %self_backward.1 = bf16[8,3,256,128]{3,2,1,0:T(8,128)(2,1)} custom-call(bf16[8,3,256,128]{3,2,1,0:T(8,128)(2,1)} %all-to-all-done.query_ref.key_ref.value_ref, bf16[8,3,256,128]{3,2,1,0:T(8,128)(2,1)} %all-to-all-done.query_ref.key_ref.value_ref, bf16[8,3,256,128]{3,2,1,0:T(8,128)(2,1)} %all-to-all-done.query_ref.key_ref.value_ref, ...), custom_call_target="tpu_custom_call" | custom-call | tf_op jit(solution)/shard_map/self_backward/pallas_call | solution.py:307
  474.5 4.6 all-to-all-start.3
  487.2 2.7 convolution_convert_fusion.10
  489.8 25.4 %all-to-all-done.3 = bf16[8,3,256,128]{3,2,1,0:T(8,128)(2,1)} async-done(((bf16[8,3,256,128]{3,2,1,0:T(8,128)(2,1)}), bf16[8,3,256,128]{3,2,1,0:T(8,128)(2,1)}, u32[]{:S(2)}, u32[]{:S(2)}) %all-to-all-start.3) | async-done | bytes 1572896 | tf_op jit(solution)/shard_map/all_to_all | solution.py:788
  515.2 2.2 slice_bitcast_fusion
  517.4 1.9 copy.177
  522.7 2.0 copy.175
  524.7 2.1 fusion.90
  528.4 2.1 fusion.39
  531.7 1.9 pack_vectors.1
  533.6 1.7 convolution_convert_fusion.13
  538.4 2.1 constant_dynamic-slice_fusion.1
  540.5 1.9 copy.244
  542.5 6.3 collective-permute-done.6
  548.7 3.9 fusion
  560.6 17.4 %collective-permute-done.7 = bf16[2,2,2,64,768]{4,3,0,1,2:T(8,128)(2,1)} collective-permute-done((bf16[2,2,2,64,768]{4,3,0,1,2:T(8,128)(2,1)}, bf16[2,2,2,64,768]{4,3,0,1,2:T(8,128)(2,1)}, u32[]{:S(2)}, u32[]{:S(2)}) %collective-permute-start.7) | collective-permute-done | bytes 786464 | tf_op jit(solution)/shard_map/ppermute | solution.py:412
  580.6 9.6 %collective-permute-done.9 = bf16[2,2,2,72,768]{4,3,1,2,0:T(8,128)(2,1)} collective-permute-done((bf16[2,2,2,72,768]{4,3,1,2,0:T(8,128)(2,1)}, bf16[2,2,2,72,768]{4,3,1,2,0:T(8,128)(2,1)}, u32[]{:S(2)}, u32[]{:S(2)}) %collective-permute-start.9) | collective-permute-done | bytes 884768 | tf_op jit(solution)/shard_map/ppermute | solution.py:412
  591.8 4.5 fusion.23
  596.4 2.9 collective-permute-done.8
  600.4 13.2 %collective-permute-done.11 = bf16[2,136,768]{2,1,0:T(8,128)(2,1)S(1)} collective-permute-done((bf16[2,136,768]{2,1,0:T(8,128)(2,1)S(1)}, bf16[2,136,768]{2,1,0:T(8,128)(2,1)S(1)}, u32[]{:S(2)}, u32[]{:S(2)}) %collective-permute-start.11) | collective-permute-done | bytes 417824 | tf_op jit(solution)/shard_map/ppermute | solution.py:412
  614.4 2.1 collective-permute-start.12
  616.9 1.7 copy.185
  618.6 5.3 widen_frames.1
  623.9 11.1 %collective-permute-done.12 = bf16[136,768]{1,0:T(8,128)(2,1)} collective-permute-done((bf16[136,768]{1,0:T(8,128)(2,1)}, bf16[136,768]{1,0:T(8,128)(2,1)}, u32[]{:S(2)}, u32[]{:S(2)}) %collective-permute-start.12) | collective-permute-done | bytes 208928 | tf_op jit(solution)/shard_map/ppermute | solution.py:412
  (375 shorter events, 117.4 us)
Async XLA Ops:
  7.2 213.1 %copy-start = (bf16[1536,1,768]{2,0,1:T(8,128)(2,1)S(1)}, bf16[1536,1,768]{2,0,1:T(8,128)(2,1)}, u32[]{:S(2)}) copy-start(bf16[1536,1,768]{2,0,1:T(8,128)(2,1)} %param.30) | copy-start | bytes 7077892
  7.2 87.6 %all-gather.8.cloned.1.call-start = ((), (), s32[]{:S(2)}) async-start(), calls=%async_computation.7 | async-start | bytes 6893568 | tf_op jit(solution)/shard_map/all_gather | solution.py:580
  21.4 216.0 %all-gather.10.cloned.1.call-start = ((), (), s32[]{:S(2)}) async-start(), calls=%async_computation.8 | async-start | bytes 13381632 | tf_op jit(solution)/shard_map/all_gather | solution.py:603
  25.6 69.2 %copy-start.48 = (bf16[264,768]{1,0:T(8,128)(2,1)}, bf16[264,768]{1,0:T(8,128)(2,1)S(1)}, u32[]{:S(2)}) copy-start(bf16[264,768]{1,0:T(8,128)(2,1)S(1)} %constant_dynamic-update-slice_fusion.6) | copy-start | bytes 1216516
  96.0 16.0 %copy-start.65 = (f32[256]{0:T(256)}, f32[256]{0:T(256)S(1)}, u32[]{:S(2)}) copy-start(f32[256]{0:T(256)S(1)} %broadcast_multiply_fusion.8) | copy-start | bytes 3076
  97.2 14.8 %copy-start.70 = (f32[256]{0:T(256)}, f32[256]{0:T(256)S(1)}, u32[]{:S(2)}) copy-start(f32[256]{0:T(256)S(1)} %add_rsqrt_fusion.2) | copy-start | bytes 3076
  100.8 11.2 %copy-start.73 = (f32[768]{0:T(1024)}, f32[768]{0:T(1024)S(1)}, u32[]{:S(2)}) copy-start(f32[768]{0:T(1024)S(1)} %reshape.720) | copy-start | bytes 9220
  100.9 11.1 %copy-start.53 = (f32[768]{0:T(1024)}, f32[768]{0:T(1024)S(1)}, u32[]{:S(2)}) copy-start(f32[768]{0:T(1024)S(1)} %reshape.719) | copy-start | bytes 9220
  100.9 6.1 copy-start.14
  119.6 6.5 copy-start.16
  120.9 6.6 %copy-start.83 = (s32[1,3]{1,0:T(1,128)S(1)}, s32[1,3]{1,0:T(1,128)}, u32[]{:S(2)}) copy-start(s32[1,3]{1,0:T(1,128)} %param.31) | copy-start | bytes 40
  120.9 71.3 %all-to-all-start = ((bf16[8,3,256,128]{3,2,1,0:T(8,128)(2,1)}), bf16[8,3,256,128]{3,2,1,0:T(8,128)(2,1)}, u32[]{:S(2)}, u32[]{:S(2)}) async-start(bf16[8,3,256,128]{3,2,1,0:T(8,128)(2,1)} %pad_maximum_fusion), calls=%async_computation | async-start | bytes 3145728 | tf_op jit(solution)/shard_map/all_to_all | solution.py:646
  127.6 64.5 %copy-start.52 = (s32[2048]{0:T(1024)}, s32[2048]{0:T(1024)S(1)}, u32[]{:S(2)}) copy-start(s32[2048]{0:T(1024)S(1)} %fusion.65) | copy-start | bytes 24580
  215.3 19.4 %all-to-all-start.1 = ((bf16[8,256,128]{2,1,0:T(8,128)(2,1)}), bf16[8,256,128]{2,1,0:T(8,128)(2,1)S(1)}, u32[]{:S(2)}, u32[]{:S(2)}) async-start(bf16[8,256,128]{2,1,0:T(8,128)(2,1)} %get-tuple-element.35), calls=%async_computation.1 | async-start | bytes 1048576 | tf_op jit(solution)/shard_map/all_to_all | solution.py:655
  220.1 398.5 %all-gather.6.cloned.1.call-start = ((), (), s32[]{:S(2)}) async-start(), calls=%async_computation.5 | async-start | bytes 2654208 | tf_op jit(solution)/shard_map/all_gather | solution.py:847
  241.1 12.6 %copy-start.7 = (bf16[32,24,768]{2,1,0:T(8,128)(2,1)}, bf16[32,24,768]{2,1,0:T(8,128)(2,1)S(1)}, u32[]{:S(2)}) copy-start(bf16[32,24,768]{2,1,0:T(8,128)(2,1)S(1)} %get-tuple-element.177) | copy-start | bytes 3538948
  254.5 13.4 %copy-start.68 = (f32[256]{0:T(256)}, f32[256]{0:T(256)S(1)}, u32[]{:S(2)}) copy-start(f32[256]{0:T(256)S(1)} %add_rsqrt_fusion.1) | copy-start | bytes 3076
  256.2 11.7 %copy-start.59 = (f32[768]{0:T(1024)S(1)}, f32[768]{0:T(1024)}, u32[]{:S(2)}) copy-start(f32[768]{0:T(1024)} %reshape.728) | copy-start | bytes 9220
  269.9 16.4 %copy-start.1 = (f32[256,768]{1,0:T(8,128)}, f32[256,768]{1,0:T(8,128)S(1)}, u32[]{:S(2)}) copy-start(f32[256,768]{1,0:T(8,128)S(1)} %get-tuple-element.228) | copy-start | bytes 2359300
  269.9 14.2 %slice-start = ((s8[4718592]{0:T(1024)(128)(4,1)}), s8[4194304]{0:T(1024)(128)(4,1)S(1)}, s32[]{:S(2)}) async-start(s8[4718592]{0:T(1024)(128)(4,1)} %bitcast.373), calls=%async_computation.9 | async-start | bytes 8388608
  270.1 11.1 %slice-start.2 = ((s8[4718592]{0:T(1024)(128)(4,1)}), s8[4194304]{0:T(1024)(128)(4,1)S(1)}, s32[]{:S(2)}) async-start(s8[4718592]{0:T(1024)(128)(4,1)} %bitcast.385), calls=%async_computation.11 | async-start | bytes 8388608
  270.4 10.9 %slice-start.3 = ((s8[4718592]{0:T(1024)(128)(4,1)}), s8[524288]{0:T(1024)(128)(4,1)S(1)}, s32[]{:S(2)}) async-start(s8[4718592]{0:T(1024)(128)(4,1)} %bitcast.385), calls=%async_computation.12 | async-start | bytes 1048576
  270.4 10.9 %copy-start.46 = (bf16[256,1,768]{2,1,0:T(2,128)(2,1)S(1)}, bf16[256,1,768]{2,1,0:T(2,128)(2,1)}, u32[]{:S(2)}) copy-start(bf16[256,1,768]{2,1,0:T(2,128)(2,1)} %convert_element_type.513) | copy-start | bytes 1179652
  270.4 13.7 %slice-start.1 = ((s8[4718592]{0:T(1024)(128)(4,1)}), s8[524288]{0:T(1024)(128)(4,1)S(1)}, s32[]{:S(2)}) async-start(s8[4718592]{0:T(1024)(128)(4,1)} %bitcast.373), calls=%async_computation.10 | async-start | bytes 1048576
  316.8 26.7 %collective-permute-start.3 = (bf16[2,2,192,768]{3,2,1,0:T(8,128)(2,1)}, bf16[2,2,192,768]{3,2,1,0:T(8,128)(2,1)}, u32[]{:S(2)}, u32[]{:S(2)}) collective-permute-start(bf16[2,2,192,768]{3,2,1,0:T(8,128)(2,1)} %dynamic-slice_bitcast_fusion), channel_id=1, source_target_pairs={{0,2},{1,3},{2,0},{3,1},{4,6},{5,7},{6,4},{7,5},{8,10},{9,11},{10,... | collective-permute-start | bytes 3538952 | tf_op jit(solution)/shard_map/ppermute | solution.py:412
  320.0 27.6 %collective-permute-start = (bf16[2,2,192,768]{3,2,1,0:T(8,128)(2,1)}, bf16[2,2,192,768]{3,2,1,0:T(8,128)(2,1)}, u32[]{:S(2)}, u32[]{:S(2)}) collective-permute-start(bf16[2,2,192,768]{3,2,1,0:T(8,128)(2,1)} %dynamic-slice_bitcast_fusion.1), channel_id=1, source_target_pairs={{0,1},{1,0},{2,3},{3,2},{4,5},{5,4},{6,7},{7,6},{8,9},{9,8},{10,11... | collective-permute-start | bytes 3538952 | tf_op jit(solution)/shard_map/ppermute | solution.py:412
  320.7 26.9 %copy-start.9 = (bf16[1,1536,768]{2,1,0:T(8,128)(2,1)S(1)}, bf16[1,1536,768]{2,1,0:T(8,128)(2,1)}, u32[]{:S(2)}) copy-start(bf16[1,1536,768]{2,1,0:T(8,128)(2,1)} %get-tuple-element.198) | copy-start | bytes 7077892
  345.4 13.9 %collective-permute-start.4 = (bf16[2,192,768]{2,1,0:T(8,128)(2,1)S(1)}, bf16[2,192,768]{2,1,0:T(8,128)(2,1)S(1)}, u32[]{:S(2)}, u32[]{:S(2)}) collective-permute-start(bf16[2,192,768]{2,1,0:T(8,128)(2,1)S(1)} %dynamic-slice_bitcast_fusion.4), channel_id=1, source_target_pairs={{0,1},{1,0},{2,3},{3,2},{4,5},{5,4},{6,7},{7,6},{8,9},{9,8},{10,11... | collective-permute-start | bytes 1769480 | tf_op jit(solution)/shard_map/ppermute | solution.py:412
  349.2 15.4 %collective-permute-start.1 = (bf16[2,192,768]{2,1,0:T(8,128)(2,1)S(1)}, bf16[2,192,768]{2,1,0:T(8,128)(2,1)S(1)}, u32[]{:S(2)}, u32[]{:S(2)}) collective-permute-start(bf16[2,192,768]{2,1,0:T(8,128)(2,1)S(1)} %dynamic-slice_bitcast_fusion.5), channel_id=1, source_target_pairs={{0,2},{1,3},{2,0},{3,1},{4,6},{5,7},{6,4},{7,5},{8,10},{9,11},{10,... | collective-permute-start | bytes 1769480 | tf_op jit(solution)/shard_map/ppermute | solution.py:412
  352.8 29.4 %copy-start.22 = (bf16[32,24,768]{2,1,0:T(8,128)(2,1)S(1)}, bf16[32,24,768]{2,1,0:T(8,128)(2,1)}, u32[]{:S(2)}) copy-start(bf16[32,24,768]{2,1,0:T(8,128)(2,1)} %get-tuple-element.193) | copy-start | bytes 3538948
  359.5 27.9 %copy-start.20 = (bf16[32,24,768]{2,1,0:T(8,128)(2,1)S(1)}, bf16[32,24,768]{2,1,0:T(8,128)(2,1)}, u32[]{:S(2)}) copy-start(bf16[32,24,768]{2,1,0:T(8,128)(2,1)} %get-tuple-element.197) | copy-start | bytes 3538948
  359.5 22.6 %collective-permute-start.5 = (bf16[192,768]{1,0:T(8,128)(2,1)S(1)}, bf16[192,768]{1,0:T(8,128)(2,1)S(1)}, u32[]{:S(2)}, u32[]{:S(2)}) collective-permute-start(bf16[192,768]{1,0:T(8,128)(2,1)S(1)} %dynamic-slice_bitcast_fusion.8), channel_id=1, source_target_pairs={{0,4},{1,5},{2,6},{3,7},{4,0},{5,1},{6,2},{7,3},{8,12},{9,13},{10,... | collective-permute-start | bytes 884744 | tf_op jit(solution)/shard_map/ppermute | solution.py:412
  364.7 21.9 %copy-start.26 = (bf16[2,192,768]{2,1,0:T(8,128)(2,1)}, bf16[2,192,768]{2,1,0:T(8,128)(2,1)S(1)}, u32[]{:S(2)}) copy-start(bf16[2,192,768]{2,1,0:T(8,128)(2,1)S(1)} %fusion.25) | copy-start | bytes 1769476
  364.8 21.9 %collective-permute-start.2 = (bf16[192,768]{1,0:T(8,128)(2,1)S(1)}, bf16[192,768]{1,0:T(8,128)(2,1)S(1)}, u32[]{:S(2)}, u32[]{:S(2)}) collective-permute-start(bf16[192,768]{1,0:T(8,128)(2,1)S(1)} %dynamic-slice_bitcast_fusion.9), channel_id=1, source_target_pairs={{0,4},{1,5},{2,6},{3,7},{4,0},{5,1},{6,2},{7,3},{8,12},{9,13},{10,... | collective-permute-start | bytes 884744 | tf_op jit(solution)/shard_map/ppermute | solution.py:412
  388.7 249.1 %reduce-scatter.2.cloned.1.call-start = ((), (), s32[]{:S(2)}) async-start(), calls=%async_computation.6 | async-start | bytes 13381632 | tf_op jit(solution)/shard_map/reduce_scatter | solution.py:773
  474.4 5.3 copy-start.80
  474.4 5.9 copy-start.62
  474.5 6.5 %copy-start.63 = (f32[768]{0:T(1024)S(1)}, f32[768]{0:T(1024)}, u32[]{:S(2)}) copy-start(f32[768]{0:T(1024)} %get-tuple-element.169) | copy-start | bytes 9220
  474.5 7.1 %copy-start.61 = (f32[768]{0:T(1024)S(1)}, f32[768]{0:T(1024)}, u32[]{:S(2)}) copy-start(f32[768]{0:T(1024)} %get-tuple-element.206) | copy-start | bytes 9220
  474.5 7.7 %copy-start.79 = (f32[768]{0:T(1024)S(1)}, f32[768]{0:T(1024)}, u32[]{:S(2)}) copy-start(f32[768]{0:T(1024)} %get-tuple-element.163) | copy-start | bytes 9220
  474.5 8.3 %copy-start.77 = (f32[768]{0:T(1024)S(1)}, f32[768]{0:T(1024)}, u32[]{:S(2)}) copy-start(f32[768]{0:T(1024)} %get-tuple-element.162) | copy-start | bytes 9220
  474.5 11.1 %copy-start.33 = (bf16[192,768]{1,0:T(8,128)(2,1)S(1)}, bf16[192,768]{1,0:T(8,128)(2,1)}, u32[]{:S(2)}) copy-start(bf16[192,768]{1,0:T(8,128)(2,1)} %copy-done.32) | copy-start | bytes 884740
  474.5 40.7 %all-to-all-start.3 = ((bf16[8,3,256,128]{3,2,1,0:T(8,128)(2,1)}), bf16[8,3,256,128]{3,2,1,0:T(8,128)(2,1)}, u32[]{:S(2)}, u32[]{:S(2)}) async-start(bf16[8,3,256,128]{3,2,1,0:T(8,128)(2,1)} %self_backward.1), calls=%async_computation.3 | async-start | bytes 3145728 | tf_op jit(solution)/shard_map/all_to_all | solution.py:788
  522.7 5.6 copy-start.15
  522.7 5.6 copy-start.54
  522.7 5.6 copy-start.66
  522.7 5.6 copy-start.71
  526.8 6.8 %copy-start.74 = (f32[768]{0:T(1024)S(1)}, f32[768]{0:T(1024)}, u32[]{:S(2)}) copy-start(f32[768]{0:T(1024)} %copy-done.73) | copy-start | bytes 9220
  542.5 6.3 collective-permute-start.6
  554.2 23.8 %collective-permute-start.7 = (bf16[2,2,2,64,768]{4,3,0,1,2:T(8,128)(2,1)}, bf16[2,2,2,64,768]{4,3,0,1,2:T(8,128)(2,1)}, u32[]{:S(2)}, u32[]{:S(2)}) collective-permute-start(bf16[2,2,2,64,768]{4,3,0,1,2:T(8,128)(2,1)} %dynamic-slice_bitcast_fusion.3), channel_id=1, source_target_pairs={{0,16},{8,24},{16,0},{24,8},{1,17},{9,25},{17,1},{25,9},{2,18},{10... | collective-permute-start | bytes 2359304 | tf_op jit(solution)/shard_map/ppermute | solution.py:412
  557.7 32.5 %collective-permute-start.9 = (bf16[2,2,2,72,768]{4,3,1,2,0:T(8,128)(2,1)}, bf16[2,2,2,72,768]{4,3,1,2,0:T(8,128)(2,1)}, u32[]{:S(2)}, u32[]{:S(2)}) collective-permute-start(bf16[2,2,2,72,768]{4,3,1,2,0:T(8,128)(2,1)} %dynamic-slice_bitcast_fusion.2), channel_id=1, source_target_pairs={{0,1},{1,0},{2,3},{3,2},{4,5},{5,4},{6,7},{7,6},{8,9},{9,8},{10,11... | collective-permute-start | bytes 2654216 | tf_op jit(solution)/shard_map/ppermute | solution.py:412
  560.6 29.7 %copy-start.12 = (bf16[2,2,2,2,72,768]{5,4,1,2,0,3:T(8,128)(2,1)S(1)}, bf16[2,2,2,2,72,768]{5,4,1,2,0,3:T(8,128)(2,1)}, u32[]{:S(2)}) copy-start(bf16[2,2,2,2,72,768]{5,4,1,2,0,3:T(8,128)(2,1)} %copy-done.11) | copy-start | bytes 5308420
  560.6 31.2 %copy-start.2 = (f32[256,768]{1,0:T(8,128)S(1)}, f32[256,768]{1,0:T(8,128)}, u32[]{:S(2)}) copy-start(f32[256,768]{1,0:T(8,128)} %copy-done.1) | copy-start | bytes 2359300
  560.6 31.2 %copy-start.30 = (bf16[256,3072]{1,0:T(8,128)(2,1)S(1)}, bf16[256,3072]{1,0:T(8,128)(2,1)}, u32[]{:S(2)}) copy-start(bf16[256,3072]{1,0:T(8,128)(2,1)} %get-tuple-element.171) | copy-start | bytes 4718596
  560.6 31.2 %copy-start.76 = (f32[768]{0:T(1024)S(1)}, f32[768]{0:T(1024)}, u32[]{:S(2)}) copy-start(f32[768]{0:T(1024)} %reshape.732) | copy-start | bytes 9220
  579.6 19.7 %collective-permute-start.8 = (bf16[2,2,64,768]{3,2,0,1:T(8,128)(2,1)S(1)}, bf16[2,2,64,768]{3,2,0,1:T(8,128)(2,1)S(1)}, u32[]{:S(2)}, u32[]{:S(2)}) collective-permute-start(bf16[2,2,64,768]{3,2,0,1:T(8,128)(2,1)S(1)} %dynamic-slice_bitcast_fusion.7), channel_id=1, source_target_pairs={{0,1},{1,0},{2,3},{3,2},{4,5},{5,4},{6,7},{7,6},{8,9},{9,8},{10,11... | collective-permute-start | bytes 1179656 | tf_op jit(solution)/shard_map/ppermute | solution.py:412
  591.7 8.4 %collective-permute-start.10 = (bf16[2,2,72,768]{3,2,0,1:T(8,128)(2,1)S(1)}, bf16[2,2,72,768]{3,2,0,1:T(8,128)(2,1)S(1)}, u32[]{:S(2)}, u32[]{:S(2)}) collective-permute-start(bf16[2,2,72,768]{3,2,0,1:T(8,128)(2,1)S(1)} %dynamic-slice_bitcast_fusion.6), channel_id=1, source_target_pairs={{0,16},{8,24},{16,0},{24,8},{1,17},{9,25},{17,1},{25,9},{2,18},{10... | collective-permute-start | bytes 1327112 | tf_op jit(solution)/shard_map/ppermute | solution.py:412
  596.3 20.2 %copy-start.47 = (f32[256,768]{1,0:T(8,128)S(1)}, f32[256,768]{1,0:T(8,128)}, u32[]{:S(2)}) copy-start(f32[256,768]{1,0:T(8,128)} %get-tuple-element.232) | copy-start | bytes 2359300
  596.3 20.2 %copy-start.55 = (f32[768]{0:T(1024)S(1)}, f32[768]{0:T(1024)}, u32[]{:S(2)}) copy-start(f32[768]{0:T(1024)} %copy-done.53) | copy-start | bytes 9220
  596.3 20.2 %copy-start.67 = (f32[256]{0:T(256)S(1)}, f32[256]{0:T(256)}, u32[]{:S(2)}) copy-start(f32[256]{0:T(256)} %copy-done.65) | copy-start | bytes 3076
  596.4 20.2 %copy-start.72 = (f32[256]{0:T(256)S(1)}, f32[256]{0:T(256)}, u32[]{:S(2)}) copy-start(f32[256]{0:T(256)} %copy-done.70) | copy-start | bytes 3076
  600.2 13.3 %collective-permute-start.11 = (bf16[2,136,768]{2,1,0:T(8,128)(2,1)S(1)}, bf16[2,136,768]{2,1,0:T(8,128)(2,1)S(1)}, u32[]{:S(2)}, u32[]{:S(2)}) collective-permute-start(bf16[2,136,768]{2,1,0:T(8,128)(2,1)S(1)} %fusion.49), channel_id=1, source_target_pairs={{0,2},{1,3},{2,0},{3,1},{4,6},{5,7},{6,4},{7,5},{8,10},{9,11},{10,... | collective-permute-start | bytes 1253384 | tf_op jit(solution)/shard_map/ppermute | solution.py:412
  614.4 20.5 %collective-permute-start.12 = (bf16[136,768]{1,0:T(8,128)(2,1)}, bf16[136,768]{1,0:T(8,128)(2,1)}, u32[]{:S(2)}, u32[]{:S(2)}) collective-permute-start(bf16[136,768]{1,0:T(8,128)(2,1)} %dynamic-slice_bitcast_fusion.10), channel_id=1, source_target_pairs={{0,4},{1,5},{2,6},{3,7},{4,0},{5,1},{6,2},{7,3},{8,12},{9,13},{10,... | collective-permute-start | bytes 626696 | tf_op jit(solution)/shard_map/ppermute | solution.py:412
  618.6 16.4 %copy-start.35 = (bf16[2,136,768]{2,1,0:T(8,128)(2,1)S(1)}, bf16[2,136,768]{2,1,0:T(8,128)(2,1)}, u32[]{:S(2)}) copy-start(bf16[2,136,768]{2,1,0:T(8,128)(2,1)} %copy-done.34) | copy-start | bytes 1253380
  (44 other events, 97.8 us)
Sparse Core Ops, SparseCore 0:
  21.5 73.2 all-gather.7
  97.7 117.7 all-gather.9
  388.8 62.1 all-gather.5
  456.8 179.2 reduce-scatter.1

commit v2 on v1

--- a/solution.py
+++ b/solution.py
@@ -733,8 +733,10 @@
     core_bit, x_bit = dp_index % 2, dp_index // 2
     y_bit, low_bit, high_bit = seq_index % 2, (seq_index // 2) % 2, seq_index // 4
     memory_parts = grad_memory_kv.reshape(2, 2, 2, 2, frame_part, D)
-    part_keys = halve(halve(memory_parts[0], 2, "seq", 1, y_bit), 1, "seq", 2, low_bit)
-    part_values = halve(halve(memory_parts[1], 1, "seq", 2, low_bit), 1, "seq", 1, y_bit)
+    key_columns = halve(memory_parts[0], 2, "seq", 1, y_bit)
+    value_columns = halve(memory_parts[1], 1, "seq", 2, low_bit)
+    part_keys = halve(key_columns, 1, "seq", 2, low_bit)
+    part_values = halve(value_columns, 1, "seq", 1, y_bit)
     part_flat_keys = halve(part_keys, 0, "seq", 4, high_bit)
     part_flat_values = halve(part_values, 0, "seq", 4, high_bit)
     part_memory_grad = (

time: 658 us -> 658 us (level)
  no operation moved by 1% of the time
where the time goes in v2:
time: 658 us; the launch traced here: 649 us
  waiting for transfers between devices  265 us (40%)
  local copies, waits for them, and re-layouts  118 us (18%)
  Pallas kernels  89 us (14%)
  matrix products  64.7 us (10%)
  blocking collectives  35.3 us (5%)
  other arithmetic  31.2 us (5%)
  starting transfers between devices  30 us (5%)
  between operations  16 us (2%)
    ppermute x13, waiting for transfers between devices, halve(): received = lax.ppermute(sent, axis_name, pairs)  112 us
    all_gather x1, waiting for transfers between devices, local_heads(): first = lax.all_gather(first_packed, ('dp', 'seq'), axis=0, tiled=False)  69.2 us
    all_to_all x1, waiting for transfers between devices, local_heads(): lax.all_to_all(jnp.stack(tuple((to_pairs(rows, seq_count) for rows in (qu...  52.1 us
    all_to_all x1, blocking collectives, local_heads(): head_grad = lax.all_to_all(head_blocks, 'seq', 0, 0)  35.3 us
    unnamed x202, local copies, waits for them, and re-layouts  33.4 us
    dot_general x10, matrix products, project(): return jnp.dot(left_rows, matrix, preferred_element_type=jnp.float32)  32.4 us
    pallas_call x1, Pallas kernels, self_backward(): pl.pallas_call(self_backward_body, grid=(owners,), in_specs=exchange_spec...  26.2 us
    all_to_all x1, waiting for transfers between devices, local_heads(): grad_triple = lax.all_to_all(grad_blocks, 'seq', 0, 0)  25.4 us
  transfers between devices with their start and end apart: 20, of which 16 were waited for; matrix products, arithmetic and copies ran while one was open for 22% of the time, Pallas kernels for 9%

profile of v2, /device:TPU:0, one launch (start us, length us, event | category | flops | bytes accessed | tf_op | source)
XLA Modules:
  0.0 648.6 jit_solution(13460573362990349339)
XLA Ops:
  25.6 69.2 %all-gather.8.cloned.1.call-done = bf16[4352,768]{1,0:T(8,128)(2,1)} async-done(((bf16[136,768]{1,0:T(8,128)(2,1)}), bf16[4352,768]{1,0:T(8,128)(2,1)}) %all-gather.8.cloned.1.call-update) | async-done | bytes 6684688 | tf_op jit(solution)/shard_map/all_gather | solution.py:580
  97.3 2.7 fusion.84
  100.9 5.1 fusion.85
  108.0 1.8 fusion.19
  112.0 2.6 convolution_convert_fusion.16
  114.6 1.9 copy.152
  116.5 1.9 copy.153
  120.9 4.4 all-to-all-start
  140.0 52.1 %all-to-all-done.query_ref.key_ref.value_ref = bf16[8,3,256,128]{3,2,1,0:T(8,128)(2,1)} async-done(((bf16[8,3,256,128]{3,2,1,0:T(8,128)(2,1)}), bf16[8,3,256,128]{3,2,1,0:T(8,128)(2,1)}, u32[]{:S(2)}, u32[]{:S(2)}) %all-to-all-start) | async-done | bytes 1572896 | tf_op jit(solution)/shard_map/all_to_all | solution.py:646
  192.2 23.1 %self_forward.1 = (f32[2048,128]{1,0:T(8,128)}, f32[2048,128]{1,0:T(8,128)}, bf16[8,256,128]{2,1,0:T(8,128)(2,1)}) custom-call(bf16[8,3,256,128]{3,2,1,0:T(8,128)(2,1)} %all-to-all-done.query_ref.key_ref.value_ref, bf16[8,3,256,128]{3,2,1,0:T(8,128)(2,1)} %all-to-all-done.query_ref.key_ref.value_ref, ...), custom_call_target="tpu_custom_call" | custom-call | tf_op jit(solution)/shard_map/self_forward/pallas_call | solution.py:210
  215.3 4.8 all-to-all-start.1
  220.3 4.8 fusion.7.key_ref
  225.1 3.4 fusion.8.value_ref
  228.5 6.2 all-to-all-done.1
  235.5 1.9 copy.158
  237.4 3.7 fusion.83
  241.1 7.0 %fusion.82 = (bf16[32,96,768]{2,1,0:T(8,128)(2,1)}, bf16[32,96,768]{2,1,0:T(8,128)(2,1)S(1)}) fusion(bf16[32,264,768]{2,1,0:T(8,128)(2,1)} %bitcast.350), kind=kLoop, calls=%fused_computation.268 | loop fusion | bytes 18874368 | tf_op jit(solution)/shard_map/slice | solution.py:616
  248.0 2.3 copy.170
  250.4 3.2 copy.209
  256.2 11.6 %cross_forward.1 = (bf16[256,768]{1,0:T(8,128)(2,1)}, f32[256,768]{1,0:T(8,128)}) custom-call(s32[1]{0:T(128)S(6)} %copy.269.length_ref, bf16[256,768]{1,0:T(8,128)(2,1)} %fusion.21.query_ref, bf16[1536,768]{1,0:T(8,128)(2,1)} %fusion.7.key_ref, bf16[1536,768]{1,0:T(8,128)(2,1)} %fusion.8.value_ref), custom_call_target="tpu_custom_call" | custom-call | tf_op jit(solution)/shard_map/cross_forward/pallas_call | solution.py:441
  267.9 2.0 fusion.89
  270.4 10.9 %multiply_convert_fusion = (bf16[256,3072]{1,0:T(8,128)(2,1)}, f32[256,3072]{1,0:T(8,128)S(1)}, f32[256,3072]{1,0:T(8,128)S(1)}) fusion(f32[3072]{0:T(1024)S(1)} %copy-done.64, bf16[256,768]{1,0:T(8,128)(2,1)S(1)} %add_convert_fusion.2, bf16[768,3072]{1,0:T(8,128)(2,1)} %bitcast.372), kind=kOutput, calls=%fused_computation.13 | convolution fusion | flops 1259864064 | bytes 12988416 | tf_op jit(solution)/shard_map/dot_general | solution.py:26
  281.3 2.8 convert_reduce_fusion
  284.1 2.1 multiply_reduce_fusion
  289.3 20.9 %cross_backward.1 = (bf16[256,768]{1,0:T(8,128)(2,1)}, bf16[2,1536,768]{2,1,0:T(8,128)(2,1)}) custom-call(s32[1]{0:T(128)S(6)} %copy.269.length_ref, bf16[256,768]{1,0:T(8,128)(2,1)} %fusion.21.query_ref, bf16[1536,768]{1,0:T(8,128)(2,1)} %fusion.7.key_ref, bf16[1536,768]{1,0:T(8,128)(2,1)} %fusion.8.value_ref, f32[256,768]{1,0:T(8,128)} %get-tuple-element.38.log_ref, ...), custom_call_target="tpu_custom_call" | custom-call | tf_op jit(solution)/shard_map/cross_backward/pallas_call | solution.py:484
  310.2 4.1 fusion.86
  317.5 2.4 dynamic-slice_bitcast_fusion.1
  320.7 22.8 %collective-permute-done.3 = bf16[2,2,192,768]{3,2,1,0:T(8,128)(2,1)} collective-permute-done((bf16[2,2,192,768]{3,2,1,0:T(8,128)(2,1)}, bf16[2,2,192,768]{3,2,1,0:T(8,128)(2,1)}, u32[]{:S(2)}, u32[]{:S(2)}) %collective-permute-start.3) | collective-permute-done | bytes 1179680 | tf_op jit(solution)/shard_map/ppermute | solution.py:412
  343.4 1.9 fusion.9
  345.4 2.1 collective-permute-start.4
  350.3 2.5 convolution_convert_fusion.7
  352.8 6.4 collective-permute-done.4
  359.5 2.4 collective-permute-start.5
  361.9 2.6 collective-permute-done.1
  364.8 2.3 collective-permute-start.2
  367.1 15.1 %collective-permute-done.5 = bf16[192,768]{1,0:T(8,128)(2,1)S(1)} collective-permute-done((bf16[192,768]{1,0:T(8,128)(2,1)S(1)}, bf16[192,768]{1,0:T(8,128)(2,1)S(1)}, u32[]{:S(2)}, u32[]{:S(2)}) %collective-permute-start.5) | collective-permute-done | bytes 294944 | tf_op jit(solution)/shard_map/ppermute | solution.py:412
  383.0 3.7 collective-permute-done.2
  399.2 2.4 constant_dynamic-update-slice_fusion.20
  409.0 1.8 convolution_convert_fusion.14
  412.9 35.3 %all_to_all.20.grad_ref = bf16[8,256,128]{2,1,0:T(8,128)(2,1)} all-to-all(bf16[8,256,128]{2,1,0:T(8,128)(2,1)S(1)} %pad.74), channel_id=1, replica_groups=mesh['dp'=4,'seq'=8] {'seq'}, dimensions={0} | all-to-all | bytes 1048576 | tf_op jit(solution)/shard_map/all_to_all | solution.py:788
  448.3 26.2 %self_backward.1 = bf16[8,3,256,128]{3,2,1,0:T(8,128)(2,1)} custom-call(bf16[8,3,256,128]{3,2,1,0:T(8,128)(2,1)} %all-to-all-done.query_ref.key_ref.value_ref, bf16[8,3,256,128]{3,2,1,0:T(8,128)(2,1)} %all-to-all-done.query_ref.key_ref.value_ref, bf16[8,3,256,128]{3,2,1,0:T(8,128)(2,1)} %all-to-all-done.query_ref.key_ref.value_ref, ...), custom_call_target="tpu_custom_call" | custom-call | tf_op jit(solution)/shard_map/self_backward/pallas_call | solution.py:307
  474.5 4.6 all-to-all-start.3
  487.2 2.7 convolution_convert_fusion.10
  489.8 25.4 %all-to-all-done.3 = bf16[8,3,256,128]{3,2,1,0:T(8,128)(2,1)} async-done(((bf16[8,3,256,128]{3,2,1,0:T(8,128)(2,1)}), bf16[8,3,256,128]{3,2,1,0:T(8,128)(2,1)}, u32[]{:S(2)}, u32[]{:S(2)}) %all-to-all-start.3) | async-done | bytes 1572896 | tf_op jit(solution)/shard_map/all_to_all | solution.py:790
  515.2 2.2 slice_bitcast_fusion
  517.4 1.9 copy.177
  522.7 2.0 copy.175
  524.7 2.1 fusion.90
  528.4 2.1 fusion.39
  531.7 1.9 pack_vectors.1
  533.6 1.7 convolution_convert_fusion.13
  538.4 2.1 constant_dynamic-slice_fusion.1
  540.5 1.9 copy.244
  542.5 6.3 collective-permute-done.6
  548.7 3.9 fusion
  560.6 17.4 %collective-permute-done.7 = bf16[2,2,2,64,768]{4,3,0,1,2:T(8,128)(2,1)} collective-permute-done((bf16[2,2,2,64,768]{4,3,0,1,2:T(8,128)(2,1)}, bf16[2,2,2,64,768]{4,3,0,1,2:T(8,128)(2,1)}, u32[]{:S(2)}, u32[]{:S(2)}) %collective-permute-start.7) | collective-permute-done | bytes 786464 | tf_op jit(solution)/shard_map/ppermute | solution.py:412
  580.6 9.6 %collective-permute-done.9 = bf16[2,2,2,72,768]{4,3,1,2,0:T(8,128)(2,1)} collective-permute-done((bf16[2,2,2,72,768]{4,3,1,2,0:T(8,128)(2,1)}, bf16[2,2,2,72,768]{4,3,1,2,0:T(8,128)(2,1)}, u32[]{:S(2)}, u32[]{:S(2)}) %collective-permute-start.9) | collective-permute-done | bytes 884768 | tf_op jit(solution)/shard_map/ppermute | solution.py:412
  591.8 4.5 fusion.23
  596.4 2.9 collective-permute-done.8
  600.4 13.2 %collective-permute-done.11 = bf16[2,136,768]{2,1,0:T(8,128)(2,1)S(1)} collective-permute-done((bf16[2,136,768]{2,1,0:T(8,128)(2,1)S(1)}, bf16[2,136,768]{2,1,0:T(8,128)(2,1)S(1)}, u32[]{:S(2)}, u32[]{:S(2)}) %collective-permute-start.11) | collective-permute-done | bytes 417824 | tf_op jit(solution)/shard_map/ppermute | solution.py:412
  614.4 2.1 collective-permute-start.12
  616.9 1.7 copy.185
  618.6 5.3 widen_frames.1
  623.9 11.1 %collective-permute-done.12 = bf16[136,768]{1,0:T(8,128)(2,1)} collective-permute-done((bf16[136,768]{1,0:T(8,128)(2,1)}, bf16[136,768]{1,0:T(8,128)(2,1)}, u32[]{:S(2)}, u32[]{:S(2)}) %collective-permute-start.12) | collective-permute-done | bytes 208928 | tf_op jit(solution)/shard_map/ppermute | solution.py:412
  (375 shorter events, 117.4 us)
Async XLA Ops:
  7.2 213.1 %copy-start = (bf16[1536,1,768]{2,0,1:T(8,128)(2,1)S(1)}, bf16[1536,1,768]{2,0,1:T(8,128)(2,1)}, u32[]{:S(2)}) copy-start(bf16[1536,1,768]{2,0,1:T(8,128)(2,1)} %param.30) | copy-start | bytes 7077892
  7.2 87.6 %all-gather.8.cloned.1.call-start = ((), (), s32[]{:S(2)}) async-start(), calls=%async_computation.7 | async-start | bytes 6893568 | tf_op jit(solution)/shard_map/all_gather | solution.py:580
  21.4 216.0 %all-gather.10.cloned.1.call-start = ((), (), s32[]{:S(2)}) async-start(), calls=%async_computation.8 | async-start | bytes 13381632 | tf_op jit(solution)/shard_map/all_gather | solution.py:603
  25.6 69.2 %copy-start.48 = (bf16[264,768]{1,0:T(8,128)(2,1)}, bf16[264,768]{1,0:T(8,128)(2,1)S(1)}, u32[]{:S(2)}) copy-start(bf16[264,768]{1,0:T(8,128)(2,1)S(1)} %constant_dynamic-update-slice_fusion.6) | copy-start | bytes 1216516
  96.0 16.0 %copy-start.65 = (f32[256]{0:T(256)}, f32[256]{0:T(256)S(1)}, u32[]{:S(2)}) copy-start(f32[256]{0:T(256)S(1)} %broadcast_multiply_fusion.8) | copy-start | bytes 3076
  97.2 14.8 %copy-start.70 = (f32[256]{0:T(256)}, f32[256]{0:T(256)S(1)}, u32[]{:S(2)}) copy-start(f32[256]{0:T(256)S(1)} %add_rsqrt_fusion.2) | copy-start | bytes 3076
  100.8 11.2 %copy-start.73 = (f32[768]{0:T(1024)}, f32[768]{0:T(1024)S(1)}, u32[]{:S(2)}) copy-start(f32[768]{0:T(1024)S(1)} %reshape.720) | copy-start | bytes 9220
  100.9 11.1 %copy-start.53 = (f32[768]{0:T(1024)}, f32[768]{0:T(1024)S(1)}, u32[]{:S(2)}) copy-start(f32[768]{0:T(1024)S(1)} %reshape.719) | copy-start | bytes 9220
  100.9 6.1 copy-start.14
  119.6 6.5 copy-start.16
  120.9 6.6 %copy-start.83 = (s32[1,3]{1,0:T(1,128)S(1)}, s32[1,3]{1,0:T(1,128)}, u32[]{:S(2)}) copy-start(s32[1,3]{1,0:T(1,128)} %param.31) | copy-start | bytes 40
  120.9 71.3 %all-to-all-start = ((bf16[8,3,256,128]{3,2,1,0:T(8,128)(2,1)}), bf16[8,3,256,128]{3,2,1,0:T(8,128)(2,1)}, u32[]{:S(2)}, u32[]{:S(2)}) async-start(bf16[8,3,256,128]{3,2,1,0:T(8,128)(2,1)} %pad_maximum_fusion), calls=%async_computation | async-start | bytes 3145728 | tf_op jit(solution)/shard_map/all_to_all | solution.py:646
  127.6 64.5 %copy-start.52 = (s32[2048]{0:T(1024)}, s32[2048]{0:T(1024)S(1)}, u32[]{:S(2)}) copy-start(s32[2048]{0:T(1024)S(1)} %fusion.65) | copy-start | bytes 24580
  215.3 19.4 %all-to-all-start.1 = ((bf16[8,256,128]{2,1,0:T(8,128)(2,1)}), bf16[8,256,128]{2,1,0:T(8,128)(2,1)S(1)}, u32[]{:S(2)}, u32[]{:S(2)}) async-start(bf16[8,256,128]{2,1,0:T(8,128)(2,1)} %get-tuple-element.35), calls=%async_computation.1 | async-start | bytes 1048576 | tf_op jit(solution)/shard_map/all_to_all | solution.py:655
  220.1 398.5 %all-gather.6.cloned.1.call-start = ((), (), s32[]{:S(2)}) async-start(), calls=%async_computation.5 | async-start | bytes 2654208 | tf_op jit(solution)/shard_map/all_gather | solution.py:849
  241.1 12.6 %copy-start.7 = (bf16[32,24,768]{2,1,0:T(8,128)(2,1)}, bf16[32,24,768]{2,1,0:T(8,128)(2,1)S(1)}, u32[]{:S(2)}) copy-start(bf16[32,24,768]{2,1,0:T(8,128)(2,1)S(1)} %get-tuple-element.177) | copy-start | bytes 3538948
  254.5 13.4 %copy-start.68 = (f32[256]{0:T(256)}, f32[256]{0:T(256)S(1)}, u32[]{:S(2)}) copy-start(f32[256]{0:T(256)S(1)} %add_rsqrt_fusion.1) | copy-start | bytes 3076
  256.2 11.7 %copy-start.59 = (f32[768]{0:T(1024)S(1)}, f32[768]{0:T(1024)}, u32[]{:S(2)}) copy-start(f32[768]{0:T(1024)} %reshape.728) | copy-start | bytes 9220
  269.9 16.4 %copy-start.1 = (f32[256,768]{1,0:T(8,128)}, f32[256,768]{1,0:T(8,128)S(1)}, u32[]{:S(2)}) copy-start(f32[256,768]{1,0:T(8,128)S(1)} %get-tuple-element.228) | copy-start | bytes 2359300
  269.9 14.2 %slice-start = ((s8[4718592]{0:T(1024)(128)(4,1)}), s8[4194304]{0:T(1024)(128)(4,1)S(1)}, s32[]{:S(2)}) async-start(s8[4718592]{0:T(1024)(128)(4,1)} %bitcast.373), calls=%async_computation.9 | async-start | bytes 8388608
  270.1 11.1 %slice-start.2 = ((s8[4718592]{0:T(1024)(128)(4,1)}), s8[4194304]{0:T(1024)(128)(4,1)S(1)}, s32[]{:S(2)}) async-start(s8[4718592]{0:T(1024)(128)(4,1)} %bitcast.385), calls=%async_computation.11 | async-start | bytes 8388608
  270.4 10.9 %slice-start.3 = ((s8[4718592]{0:T(1024)(128)(4,1)}), s8[524288]{0:T(1024)(128)(4,1)S(1)}, s32[]{:S(2)}) async-start(s8[4718592]{0:T(1024)(128)(4,1)} %bitcast.385), calls=%async_computation.12 | async-start | bytes 1048576
  270.4 10.9 %copy-start.46 = (bf16[256,1,768]{2,1,0:T(2,128)(2,1)S(1)}, bf16[256,1,768]{2,1,0:T(2,128)(2,1)}, u32[]{:S(2)}) copy-start(bf16[256,1,768]{2,1,0:T(2,128)(2,1)} %convert_element_type.513) | copy-start | bytes 1179652
  270.4 13.7 %slice-start.1 = ((s8[4718592]{0:T(1024)(128)(4,1)}), s8[524288]{0:T(1024)(128)(4,1)S(1)}, s32[]{:S(2)}) async-start(s8[4718592]{0:T(1024)(128)(4,1)} %bitcast.373), calls=%async_computation.10 | async-start | bytes 1048576
  316.8 26.7 %collective-permute-start.3 = (bf16[2,2,192,768]{3,2,1,0:T(8,128)(2,1)}, bf16[2,2,192,768]{3,2,1,0:T(8,128)(2,1)}, u32[]{:S(2)}, u32[]{:S(2)}) collective-permute-start(bf16[2,2,192,768]{3,2,1,0:T(8,128)(2,1)} %dynamic-slice_bitcast_fusion), channel_id=1, source_target_pairs={{0,2},{1,3},{2,0},{3,1},{4,6},{5,7},{6,4},{7,5},{8,10},{9,11},{10,... | collective-permute-start | bytes 3538952 | tf_op jit(solution)/shard_map/ppermute | solution.py:412
  320.0 27.6 %collective-permute-start = (bf16[2,2,192,768]{3,2,1,0:T(8,128)(2,1)}, bf16[2,2,192,768]{3,2,1,0:T(8,128)(2,1)}, u32[]{:S(2)}, u32[]{:S(2)}) collective-permute-start(bf16[2,2,192,768]{3,2,1,0:T(8,128)(2,1)} %dynamic-slice_bitcast_fusion.1), channel_id=1, source_target_pairs={{0,1},{1,0},{2,3},{3,2},{4,5},{5,4},{6,7},{7,6},{8,9},{9,8},{10,11... | collective-permute-start | bytes 3538952 | tf_op jit(solution)/shard_map/ppermute | solution.py:412
  320.7 26.9 %copy-start.9 = (bf16[1,1536,768]{2,1,0:T(8,128)(2,1)S(1)}, bf16[1,1536,768]{2,1,0:T(8,128)(2,1)}, u32[]{:S(2)}) copy-start(bf16[1,1536,768]{2,1,0:T(8,128)(2,1)} %get-tuple-element.198) | copy-start | bytes 7077892
  345.4 13.9 %collective-permute-start.4 = (bf16[2,192,768]{2,1,0:T(8,128)(2,1)S(1)}, bf16[2,192,768]{2,1,0:T(8,128)(2,1)S(1)}, u32[]{:S(2)}, u32[]{:S(2)}) collective-permute-start(bf16[2,192,768]{2,1,0:T(8,128)(2,1)S(1)} %dynamic-slice_bitcast_fusion.4), channel_id=1, source_target_pairs={{0,1},{1,0},{2,3},{3,2},{4,5},{5,4},{6,7},{7,6},{8,9},{9,8},{10,11... | collective-permute-start | bytes 1769480 | tf_op jit(solution)/shard_map/ppermute | solution.py:412
  349.2 15.4 %collective-permute-start.1 = (bf16[2,192,768]{2,1,0:T(8,128)(2,1)S(1)}, bf16[2,192,768]{2,1,0:T(8,128)(2,1)S(1)}, u32[]{:S(2)}, u32[]{:S(2)}) collective-permute-start(bf16[2,192,768]{2,1,0:T(8,128)(2,1)S(1)} %dynamic-slice_bitcast_fusion.5), channel_id=1, source_target_pairs={{0,2},{1,3},{2,0},{3,1},{4,6},{5,7},{6,4},{7,5},{8,10},{9,11},{10,... | collective-permute-start | bytes 1769480 | tf_op jit(solution)/shard_map/ppermute | solution.py:412
  352.8 29.4 %copy-start.22 = (bf16[32,24,768]{2,1,0:T(8,128)(2,1)S(1)}, bf16[32,24,768]{2,1,0:T(8,128)(2,1)}, u32[]{:S(2)}) copy-start(bf16[32,24,768]{2,1,0:T(8,128)(2,1)} %get-tuple-element.193) | copy-start | bytes 3538948
  359.5 27.9 %copy-start.20 = (bf16[32,24,768]{2,1,0:T(8,128)(2,1)S(1)}, bf16[32,24,768]{2,1,0:T(8,128)(2,1)}, u32[]{:S(2)}) copy-start(bf16[32,24,768]{2,1,0:T(8,128)(2,1)} %get-tuple-element.197) | copy-start | bytes 3538948
  359.5 22.6 %collective-permute-start.5 = (bf16[192,768]{1,0:T(8,128)(2,1)S(1)}, bf16[192,768]{1,0:T(8,128)(2,1)S(1)}, u32[]{:S(2)}, u32[]{:S(2)}) collective-permute-start(bf16[192,768]{1,0:T(8,128)(2,1)S(1)} %dynamic-slice_bitcast_fusion.8), channel_id=1, source_target_pairs={{0,4},{1,5},{2,6},{3,7},{4,0},{5,1},{6,2},{7,3},{8,12},{9,13},{10,... | collective-permute-start | bytes 884744 | tf_op jit(solution)/shard_map/ppermute | solution.py:412
  364.7 21.9 %copy-start.26 = (bf16[2,192,768]{2,1,0:T(8,128)(2,1)}, bf16[2,192,768]{2,1,0:T(8,128)(2,1)S(1)}, u32[]{:S(2)}) copy-start(bf16[2,192,768]{2,1,0:T(8,128)(2,1)S(1)} %fusion.25) | copy-start | bytes 1769476
  364.8 21.9 %collective-permute-start.2 = (bf16[192,768]{1,0:T(8,128)(2,1)S(1)}, bf16[192,768]{1,0:T(8,128)(2,1)S(1)}, u32[]{:S(2)}, u32[]{:S(2)}) collective-permute-start(bf16[192,768]{1,0:T(8,128)(2,1)S(1)} %dynamic-slice_bitcast_fusion.9), channel_id=1, source_target_pairs={{0,4},{1,5},{2,6},{3,7},{4,0},{5,1},{6,2},{7,3},{8,12},{9,13},{10,... | collective-permute-start | bytes 884744 | tf_op jit(solution)/shard_map/ppermute | solution.py:412
  388.7 249.1 %reduce-scatter.2.cloned.1.call-start = ((), (), s32[]{:S(2)}) async-start(), calls=%async_computation.6 | async-start | bytes 13381632 | tf_op jit(solution)/shard_map/reduce_scatter | solution.py:775
  474.4 5.3 copy-start.80
  474.4 5.9 copy-start.62
  474.5 6.5 %copy-start.63 = (f32[768]{0:T(1024)S(1)}, f32[768]{0:T(1024)}, u32[]{:S(2)}) copy-start(f32[768]{0:T(1024)} %get-tuple-element.169) | copy-start | bytes 9220
  474.5 7.1 %copy-start.61 = (f32[768]{0:T(1024)S(1)}, f32[768]{0:T(1024)}, u32[]{:S(2)}) copy-start(f32[768]{0:T(1024)} %get-tuple-element.206) | copy-start | bytes 9220
  474.5 7.7 %copy-start.79 = (f32[768]{0:T(1024)S(1)}, f32[768]{0:T(1024)}, u32[]{:S(2)}) copy-start(f32[768]{0:T(1024)} %get-tuple-element.163) | copy-start | bytes 9220
  474.5 8.3 %copy-start.77 = (f32[768]{0:T(1024)S(1)}, f32[768]{0:T(1024)}, u32[]{:S(2)}) copy-start(f32[768]{0:T(1024)} %get-tuple-element.162) | copy-start | bytes 9220
  474.5 11.1 %copy-start.33 = (bf16[192,768]{1,0:T(8,128)(2,1)S(1)}, bf16[192,768]{1,0:T(8,128)(2,1)}, u32[]{:S(2)}) copy-start(bf16[192,768]{1,0:T(8,128)(2,1)} %copy-done.32) | copy-start | bytes 884740
  474.5 40.7 %all-to-all-start.3 = ((bf16[8,3,256,128]{3,2,1,0:T(8,128)(2,1)}), bf16[8,3,256,128]{3,2,1,0:T(8,128)(2,1)}, u32[]{:S(2)}, u32[]{:S(2)}) async-start(bf16[8,3,256,128]{3,2,1,0:T(8,128)(2,1)} %self_backward.1), calls=%async_computation.3 | async-start | bytes 3145728 | tf_op jit(solution)/shard_map/all_to_all | solution.py:790
  522.7 5.6 copy-start.15
  522.7 5.6 copy-start.54
  522.7 5.6 copy-start.66
  522.7 5.6 copy-start.71
  526.8 6.8 %copy-start.74 = (f32[768]{0:T(1024)S(1)}, f32[768]{0:T(1024)}, u32[]{:S(2)}) copy-start(f32[768]{0:T(1024)} %copy-done.73) | copy-start | bytes 9220
  542.5 6.3 collective-permute-start.6
  554.2 23.8 %collective-permute-start.7 = (bf16[2,2,2,64,768]{4,3,0,1,2:T(8,128)(2,1)}, bf16[2,2,2,64,768]{4,3,0,1,2:T(8,128)(2,1)}, u32[]{:S(2)}, u32[]{:S(2)}) collective-permute-start(bf16[2,2,2,64,768]{4,3,0,1,2:T(8,128)(2,1)} %dynamic-slice_bitcast_fusion.3), channel_id=1, source_target_pairs={{0,16},{8,24},{16,0},{24,8},{1,17},{9,25},{17,1},{25,9},{2,18},{10... | collective-permute-start | bytes 2359304 | tf_op jit(solution)/shard_map/ppermute | solution.py:412
  557.7 32.5 %collective-permute-start.9 = (bf16[2,2,2,72,768]{4,3,1,2,0:T(8,128)(2,1)}, bf16[2,2,2,72,768]{4,3,1,2,0:T(8,128)(2,1)}, u32[]{:S(2)}, u32[]{:S(2)}) collective-permute-start(bf16[2,2,2,72,768]{4,3,1,2,0:T(8,128)(2,1)} %dynamic-slice_bitcast_fusion.2), channel_id=1, source_target_pairs={{0,1},{1,0},{2,3},{3,2},{4,5},{5,4},{6,7},{7,6},{8,9},{9,8},{10,11... | collective-permute-start | bytes 2654216 | tf_op jit(solution)/shard_map/ppermute | solution.py:412
  560.6 29.7 %copy-start.12 = (bf16[2,2,2,2,72,768]{5,4,1,2,0,3:T(8,128)(2,1)S(1)}, bf16[2,2,2,2,72,768]{5,4,1,2,0,3:T(8,128)(2,1)}, u32[]{:S(2)}) copy-start(bf16[2,2,2,2,72,768]{5,4,1,2,0,3:T(8,128)(2,1)} %copy-done.11) | copy-start | bytes 5308420
  560.6 31.2 %copy-start.2 = (f32[256,768]{1,0:T(8,128)S(1)}, f32[256,768]{1,0:T(8,128)}, u32[]{:S(2)}) copy-start(f32[256,768]{1,0:T(8,128)} %copy-done.1) | copy-start | bytes 2359300
  560.6 31.2 %copy-start.30 = (bf16[256,3072]{1,0:T(8,128)(2,1)S(1)}, bf16[256,3072]{1,0:T(8,128)(2,1)}, u32[]{:S(2)}) copy-start(bf16[256,3072]{1,0:T(8,128)(2,1)} %get-tuple-element.171) | copy-start | bytes 4718596
  560.6 31.2 %copy-start.76 = (f32[768]{0:T(1024)S(1)}, f32[768]{0:T(1024)}, u32[]{:S(2)}) copy-start(f32[768]{0:T(1024)} %reshape.732) | copy-start | bytes 9220
  579.6 19.7 %collective-permute-start.8 = (bf16[2,2,64,768]{3,2,0,1:T(8,128)(2,1)S(1)}, bf16[2,2,64,768]{3,2,0,1:T(8,128)(2,1)S(1)}, u32[]{:S(2)}, u32[]{:S(2)}) collective-permute-start(bf16[2,2,64,768]{3,2,0,1:T(8,128)(2,1)S(1)} %dynamic-slice_bitcast_fusion.7), channel_id=1, source_target_pairs={{0,1},{1,0},{2,3},{3,2},{4,5},{5,4},{6,7},{7,6},{8,9},{9,8},{10,11... | collective-permute-start | bytes 1179656 | tf_op jit(solution)/shard_map/ppermute | solution.py:412
  591.7 8.4 %collective-permute-start.10 = (bf16[2,2,72,768]{3,2,0,1:T(8,128)(2,1)S(1)}, bf16[2,2,72,768]{3,2,0,1:T(8,128)(2,1)S(1)}, u32[]{:S(2)}, u32[]{:S(2)}) collective-permute-start(bf16[2,2,72,768]{3,2,0,1:T(8,128)(2,1)S(1)} %dynamic-slice_bitcast_fusion.6), channel_id=1, source_target_pairs={{0,16},{8,24},{16,0},{24,8},{1,17},{9,25},{17,1},{25,9},{2,18},{10... | collective-permute-start | bytes 1327112 | tf_op jit(solution)/shard_map/ppermute | solution.py:412
  596.3 20.2 %copy-start.47 = (f32[256,768]{1,0:T(8,128)S(1)}, f32[256,768]{1,0:T(8,128)}, u32[]{:S(2)}) copy-start(f32[256,768]{1,0:T(8,128)} %get-tuple-element.232) | copy-start | bytes 2359300
  596.3 20.2 %copy-start.55 = (f32[768]{0:T(1024)S(1)}, f32[768]{0:T(1024)}, u32[]{:S(2)}) copy-start(f32[768]{0:T(1024)} %copy-done.53) | copy-start | bytes 9220
  596.3 20.2 %copy-start.67 = (f32[256]{0:T(256)S(1)}, f32[256]{0:T(256)}, u32[]{:S(2)}) copy-start(f32[256]{0:T(256)} %copy-done.65) | copy-start | bytes 3076
  596.4 20.2 %copy-start.72 = (f32[256]{0:T(256)S(1)}, f32[256]{0:T(256)}, u32[]{:S(2)}) copy-start(f32[256]{0:T(256)} %copy-done.70) | copy-start | bytes 3076
  600.2 13.3 %collective-permute-start.11 = (bf16[2,136,768]{2,1,0:T(8,128)(2,1)S(1)}, bf16[2,136,768]{2,1,0:T(8,128)(2,1)S(1)}, u32[]{:S(2)}, u32[]{:S(2)}) collective-permute-start(bf16[2,136,768]{2,1,0:T(8,128)(2,1)S(1)} %fusion.49), channel_id=1, source_target_pairs={{0,2},{1,3},{2,0},{3,1},{4,6},{5,7},{6,4},{7,5},{8,10},{9,11},{10,... | collective-permute-start | bytes 1253384 | tf_op jit(solution)/shard_map/ppermute | solution.py:412
  614.4 20.5 %collective-permute-start.12 = (bf16[136,768]{1,0:T(8,128)(2,1)}, bf16[136,768]{1,0:T(8,128)(2,1)}, u32[]{:S(2)}, u32[]{:S(2)}) collective-permute-start(bf16[136,768]{1,0:T(8,128)(2,1)} %dynamic-slice_bitcast_fusion.10), channel_id=1, source_target_pairs={{0,4},{1,5},{2,6},{3,7},{4,0},{5,1},{6,2},{7,3},{8,12},{9,13},{10,... | collective-permute-start | bytes 626696 | tf_op jit(solution)/shard_map/ppermute | solution.py:412
  618.6 16.4 %copy-start.35 = (bf16[2,136,768]{2,1,0:T(8,128)(2,1)S(1)}, bf16[2,136,768]{2,1,0:T(8,128)(2,1)}, u32[]{:S(2)}) copy-start(bf16[2,136,768]{2,1,0:T(8,128)(2,1)} %copy-done.34) | copy-start | bytes 1253380
  (44 other events, 97.8 us)
Sparse Core Ops, SparseCore 0:
  21.5 73.2 all-gather.7
  97.7 117.7 all-gather.9
  388.8 62.1 all-gather.5
  456.8 179.2 reduce-scatter.1
